TPU v7x, 128 devices: a whole 4x4x4 slice. The times are simulated.
128 devices in a mesh: orbit: 32 (over y, z, core), region: 4 (over x).
Axes of the slice: x: 4, y: 4, z: 4, core: 2. Of those that a mesh axis runs over, the one named last changes fastest.
Arguments:
- footprints: bfloat16 [40960, 64, 256], P(('orbit', 'region')), may hold values from -0.0625 to 0.0625
- block_sounding: int32 [40960], P(('orbit', 'region')), may hold values from 0 to 31
- block_tile: int32 [40960], P(('orbit', 'region')), may hold values from 0 to 31
- block_count: int32 [128], P(('orbit', 'region')), may hold values from 80 to 320, as said below
- observations: float32 [1024, 64, 128], P('orbit'), may hold values from -6 to 6
- obs_weight: float32 [1024, 64], P('orbit'), may hold values from 0.25 to 4
- prior_std: float32 [4, 32, 256], P('region', 'orbit'), may hold values from 0.4 to 4.8
Outputs:
- flux: float32 [4, 32, 256, 128], P('region', 'orbit')
- residual: float32 [4, 32, 256, 128], P('region', 'orbit')
Inputs may be any that keep to these rules, and one draw needn't show every extreme that they name: `block_sounding`: index of a sounding block among the 32 of the block's orbit index. `block_tile`: index of a tile among the 32 of the block's region; some tiles are named far more often than others. `block_count`: slots from this count on are unused; some device has all 320 slots live.
All inputs are finite; a program needn't handle non-finite values.
Results may differ from a plain program's by a relative error of at most 0.0068.
Values may be sent and summed in bfloat16 or wider, within the bound.
A program may use at most 128 MiB of HBM per device.

v0:
```python
import jax
import jax.numpy as jnp
from jax import lax
from jax.sharding import PartitionSpec as P

ITERS = 2
GROUP = 64


def local_forward(footprints, block_sounding, block_tile, live_count, whole, sb_count):
    rounds = (live_count + GROUP - 1) // GROUP
    positions = jnp.arange(GROUP, dtype=jnp.int32)
    width = whole.shape[2]

    def turn(turn_index, running):
        offset = turn_index * GROUP
        blocks_now = lax.dynamic_slice_in_dim(footprints, offset, GROUP, 0)
        sound_ids = lax.dynamic_slice_in_dim(block_sounding, offset, GROUP, 0)
        tile_ids = lax.dynamic_slice_in_dim(block_tile, offset, GROUP, 0)
        alive = offset + positions < live_count
        targets = jnp.where(alive, sound_ids, sb_count)
        products = jnp.einsum(
            "bsc,bcr->bsr", blocks_now, whole[tile_ids], preferred_element_type=jnp.float32
        )
        return running + jax.ops.segment_sum(products, targets, num_segments=sb_count)

    start_sum = jnp.zeros((sb_count, footprints.shape[1], width), jnp.float32)
    return lax.fori_loop(0, rounds, turn, start_sum)


def local_transpose(footprints, block_sounding, block_tile, live_count, weighted, tile_count):
    rounds = (live_count + GROUP - 1) // GROUP
    positions = jnp.arange(GROUP, dtype=jnp.int32)
    width = weighted.shape[2]

    def turn(turn_index, running):
        offset = turn_index * GROUP
        blocks_now = lax.dynamic_slice_in_dim(footprints, offset, GROUP, 0)
        sound_ids = lax.dynamic_slice_in_dim(block_sounding, offset, GROUP, 0)
        tile_ids = lax.dynamic_slice_in_dim(block_tile, offset, GROUP, 0)
        alive = offset + positions < live_count
        targets = jnp.where(alive, tile_ids, tile_count)
        contrib = jnp.einsum(
            "bsc,bsr->bcr", blocks_now, weighted[sound_ids], preferred_element_type=jnp.float32
        )
        return running + jax.ops.segment_sum(contrib, targets, num_segments=tile_count)

    start_sum = jnp.zeros((tile_count, footprints.shape[2], width), jnp.float32)
    return lax.fori_loop(0, rounds, turn, start_sum)


def per_device(
    footprints, block_sounding, block_tile, block_count, observations, obs_weight, prior_std
):
    live_count = block_count[0]
    share_rows = prior_std.shape[1]
    tile_count = share_rows * lax.axis_size("orbit")
    sb_count = observations.shape[0]
    weight = obs_weight[:, :, None]
    prior_scale = prior_std[0][:, :, None]

    def reduce_tiles(partial_value):
        return lax.psum_scatter(partial_value, "orbit", scatter_dimension=0, tiled=True)

    def inner_sum(first_vec, second_vec):
        return lax.psum(jnp.sum(first_vec * second_vec, axis=(0, 1)), ("orbit", "region"))

    def apply_transpose(weighted):
        return reduce_tiles(
            local_transpose(
                footprints, block_sounding, block_tile, live_count, weighted, tile_count
            )
        )

    weighted0 = (weight * observations).astype(jnp.bfloat16)
    right_side = prior_scale * apply_transpose(weighted0)
    iterate = jnp.zeros_like(right_side)
    residual = right_side
    direction = right_side
    norm_now = inner_sum(residual, residual)
    for iteration in range(ITERS):
        scaled = (prior_scale * direction).astype(jnp.bfloat16)
        partial_value = local_forward(
            footprints,
            block_sounding,
            block_tile,
            live_count,
            lax.all_gather(scaled, "orbit", axis=0, tiled=True),
            sb_count,
        )
        image = lax.psum(partial_value, "region")
        weighted = (weight * image).astype(jnp.bfloat16)
        product = direction + prior_scale * apply_transpose(weighted)
        step_size = norm_now / inner_sum(direction, product)
        iterate = iterate + step_size * direction
        residual = residual - step_size * product
        if iteration + 1 < ITERS:
            norm_next = inner_sum(residual, residual)
            direction = residual + norm_next / norm_now * direction
            norm_now = norm_next
    flux = prior_scale * iterate
    return (flux[None], residual[None])


def solution(mesh):
    return jax.shard_map(
        per_device,
        mesh=mesh,
        in_specs=(
            P(("orbit", "region"), None, None),
            P(("orbit", "region")),
            P(("orbit", "region")),
            P(("orbit", "region")),
            P("orbit", None, None),
            P("orbit", None),
            P("region", "orbit", None),
        ),
        out_specs=(P("region", "orbit", None, None), P("region", "orbit", None, None)),
        check_vma=False,
    )
```

profile of v0, /device:TPU:1, one launch (start us, length us, event | category | flops | bytes accessed | tf_op | source)
XLA Modules:
  0.0 1182.9 jit_solution(10084983206093327789)
XLA Ops:
  9.5 2.5 broadcast.40.clone.1
  11.9 106.1 %while.55 = (s32[]{:T(128)}, f32[32,256,128]{2,1,0:T(8,128)}, s32[]{:T(128)}, s32[]{:T(128)}, s32[320]{0:T(512)S(1)}, /*index=5*/bf16[320,64,256]{2,1,0:T(8,128)...) while((s32[]{:T(128)}, f32[32,256,128]{2,1,0:T(8,128)}, ...), condition=%wide.region_2.3_spmd.clone, body=%wide.region_0.2_spmd.clone.sunk | while | flops 270534016 | bytes 38803376 | solution.py:49
  13.4 6.1 fusion.47
  19.5 18.9 %scatter_fusion = f32[32,256,128]{2,1,0:T(8,128)} fusion(f32[32,256,128]{2,1,0:T(8,128)} %get-tuple-element.721, s32[64]{0:T(128)S(1)} %get-tuple-element.666, f32[64,256,128]{2,1,0:T(8,128)} %fusion.47), kind=kCustom, calls=%fused_computation.5.clone.clone.1 | custom fusion | flops 2097152 | bytes 25166080 | tf_op jit(solution)/shard_map/while/body/scatter-add | solution.py:46
  39.9 6.1 fusion.47
  46.0 18.8 %scatter_fusion = f32[32,256,128]{2,1,0:T(8,128)} fusion(f32[32,256,128]{2,1,0:T(8,128)} %get-tuple-element.721, s32[64]{0:T(128)S(1)} %get-tuple-element.666, f32[64,256,128]{2,1,0:T(8,128)} %fusion.47), kind=kCustom, calls=%fused_computation.5.clone.clone.1 | custom fusion | flops 2097152 | bytes 25166080 | tf_op jit(solution)/shard_map/while/body/scatter-add | solution.py:46
  66.3 6.1 fusion.47
  72.4 18.8 %scatter_fusion = f32[32,256,128]{2,1,0:T(8,128)} fusion(f32[32,256,128]{2,1,0:T(8,128)} %get-tuple-element.721, s32[64]{0:T(128)S(1)} %get-tuple-element.666, f32[64,256,128]{2,1,0:T(8,128)} %fusion.47), kind=kCustom, calls=%fused_computation.5.clone.clone.1 | custom fusion | flops 2097152 | bytes 25166080 | tf_op jit(solution)/shard_map/while/body/scatter-add | solution.py:46
  92.7 6.1 fusion.47
  98.8 19.2 %scatter_fusion = f32[32,256,128]{2,1,0:T(8,128)} fusion(f32[32,256,128]{2,1,0:T(8,128)} %get-tuple-element.721, s32[64]{0:T(128)S(1)} %get-tuple-element.666, f32[64,256,128]{2,1,0:T(8,128)} %fusion.47), kind=kCustom, calls=%fused_computation.5.clone.clone.1 | custom fusion | flops 2097152 | bytes 25166080 | tf_op jit(solution)/shard_map/while/body/scatter-add | solution.py:46
  118.1 110.8 %reduce-scatter.4.cloned.1.call-done = f32[1,256,128]{2,1,0:T(8,128)} async-done(((f32[32,256,128]{2,1,0:T(8,128)}), f32[1,256,128]{2,1,0:T(8,128)}) %reduce-scatter.4.cloned.1.call-update) | async-done | bytes 131088 | tf_op jit(solution)/shard_map/reduce_scatter | solution.py:63
  230.6 46.2 %all-gather.3.cloned.1.call-done = bf16[32,256,128]{2,1,0:T(8,128)(2,1)} async-done(((bf16[1,256,128]{2,1,0:T(8,128)(2,1)}), bf16[32,256,128]{2,1,0:T(8,128)(2,1)}) %all-gather.3.cloned.1.call-update) | async-done | bytes 2097168 | tf_op jit(solution)/shard_map/all_gather | solution.py:88
  276.9 51.1 %while.56 = (s32[]{:T(128)}, f32[32,64,128]{2,1,0:T(8,128)S(1)}, s32[]{:T(128)}, s32[]{:T(128)}, s32[320]{0:T(512)S(1)}, /*index=5*/bf16[320,64,256]{2,1,0:T(8,1...) while((s32[]{:T(128)}, f32[32,64,128]{2,1,0:T(8,128)S(1)}, ...), condition=%wide.region_8.9_spmd.clone, body=%wide.region_6.8_spmd.clone.sunk | while | flops 268961152 | bytes 23074740 | solution.py:28
  277.7 4.6 gather_fusion.1
  282.3 3.7 fusion.50
  286.0 3.7 scatter_fusion.1
  290.4 4.6 gather_fusion.1
  295.0 3.7 fusion.50
  298.7 3.7 scatter_fusion.1
  303.2 4.6 gather_fusion.1
  307.8 3.7 fusion.50
  311.5 3.7 scatter_fusion.1
  315.9 4.6 gather_fusion.1
  320.5 3.7 fusion.50
  324.2 3.7 scatter_fusion.1
  329.1 56.0 %all-reduce.4.cloned.1.call-done = f32[32,64,128]{2,1,0:T(8,128)} async-done(((f32[32,64,128]{2,1,0:T(8,128)}), f32[32,64,128]{2,1,0:T(8,128)}) %all-reduce.4.cloned.1.call-update) | async-done | bytes 1048592 | tf_op jit(solution)/shard_map/psum | solution.py:91
  389.1 106.1 %while.57 = (s32[]{:T(128)}, f32[32,256,128]{2,1,0:T(8,128)}, s32[]{:T(128)}, s32[]{:T(128)}, s32[320]{0:T(512)S(1)}, /*index=5*/bf16[320,64,256]{2,1,0:T(8,128)...) while((s32[]{:T(128)}, f32[32,256,128]{2,1,0:T(8,128)}, ...), condition=%wide.region_12.13_spmd.clone, body=%wide.region_10.12_spmd.clone.sunk | while | flops 270534016 | bytes 38803376 | solution.py:49
  390.6 6.1 fusion.53
  396.7 18.9 %scatter_fusion.2 = f32[32,256,128]{2,1,0:T(8,128)} fusion(f32[32,256,128]{2,1,0:T(8,128)} %get-tuple-element.793, s32[64]{0:T(128)S(1)} %get-tuple-element.686, f32[64,256,128]{2,1,0:T(8,128)} %fusion.53), kind=kCustom, calls=%fused_computation.7.clone.clone.1 | custom fusion | flops 2097152 | bytes 25166080 | tf_op jit(solution)/shard_map/while/body/scatter-add | solution.py:46
  417.1 6.1 fusion.53
  423.2 18.8 %scatter_fusion.2 = f32[32,256,128]{2,1,0:T(8,128)} fusion(f32[32,256,128]{2,1,0:T(8,128)} %get-tuple-element.793, s32[64]{0:T(128)S(1)} %get-tuple-element.686, f32[64,256,128]{2,1,0:T(8,128)} %fusion.53), kind=kCustom, calls=%fused_computation.7.clone.clone.1 | custom fusion | flops 2097152 | bytes 25166080 | tf_op jit(solution)/shard_map/while/body/scatter-add | solution.py:46
  443.4 6.1 fusion.53
  449.6 18.8 %scatter_fusion.2 = f32[32,256,128]{2,1,0:T(8,128)} fusion(f32[32,256,128]{2,1,0:T(8,128)} %get-tuple-element.793, s32[64]{0:T(128)S(1)} %get-tuple-element.686, f32[64,256,128]{2,1,0:T(8,128)} %fusion.53), kind=kCustom, calls=%fused_computation.7.clone.clone.1 | custom fusion | flops 2097152 | bytes 25166080 | tf_op jit(solution)/shard_map/while/body/scatter-add | solution.py:46
  469.8 6.1 fusion.53
  475.9 19.2 %scatter_fusion.2 = f32[32,256,128]{2,1,0:T(8,128)} fusion(f32[32,256,128]{2,1,0:T(8,128)} %get-tuple-element.793, s32[64]{0:T(128)S(1)} %get-tuple-element.686, f32[64,256,128]{2,1,0:T(8,128)} %fusion.53), kind=kCustom, calls=%fused_computation.7.clone.clone.1 | custom fusion | flops 2097152 | bytes 25166080 | tf_op jit(solution)/shard_map/while/body/scatter-add | solution.py:46
  495.2 110.0 %reduce-scatter.6.cloned.1.call-done = f32[1,256,128]{2,1,0:T(8,128)} async-done(((f32[32,256,128]{2,1,0:T(8,128)}), f32[1,256,128]{2,1,0:T(8,128)}) %reduce-scatter.6.cloned.1.call-update) | async-done | bytes 131088 | tf_op jit(solution)/shard_map/reduce_scatter | solution.py:63
  606.3 65.9 %all-reduce = (f32[128]{0:T(128)S(1)}, f32[128]{0:T(128)S(1)}) all-reduce(f32[128]{0:T(128)S(1)} %get-tuple-element.343, f32[128]{0:T(128)S(1)} %get-tuple-element.342), channel_id=1, replica_groups=mesh['orbit'=32,'region'=4] {'orbit','region'}, use_global_device_ids=true, to_apply=%region_5.6 | all-reduce | flops 256 | bytes 2048 | tf_op jit(solution)/shard_map/psum | solution.py:66
  673.2 62.7 %psum.45 = f32[128]{0:T(128)S(1)} all-reduce(f32[128]{0:T(128)S(1)} %multiply_reduce_fusion.1), channel_id=1, replica_groups=mesh['orbit'=32,'region'=4] {'orbit','region'}, use_global_device_ids=true, to_apply=%region_17.18 | all-reduce | flops 128 | bytes 1024 | tf_op jit(solution)/shard_map/psum | solution.py:66
  737.6 41.3 %all-gather.5.cloned.1.call-done = bf16[32,256,128]{2,1,0:T(8,128)(2,1)} async-done(((bf16[1,256,128]{2,1,0:T(8,128)(2,1)}), bf16[32,256,128]{2,1,0:T(8,128)(2,1)}) %all-gather.5.cloned.1.call-update) | async-done | bytes 2097168 | tf_op jit(solution)/shard_map/all_gather | solution.py:88
  779.1 51.1 %while.58 = (s32[]{:T(128)}, f32[32,64,128]{2,1,0:T(8,128)S(1)}, s32[]{:T(128)}, s32[]{:T(128)}, s32[320]{0:T(512)S(1)}, /*index=5*/bf16[320,64,256]{2,1,0:T(8,1...) while((s32[]{:T(128)}, f32[32,64,128]{2,1,0:T(8,128)S(1)}, ...), condition=%wide.region_20.21_spmd.clone, body=%wide.region_18.20_spmd.clone.sunk | while | flops 268961152 | bytes 23074740 | solution.py:28
  779.8 4.6 gather_fusion.3
  784.4 3.7 fusion.56
  788.1 3.7 scatter_fusion.3
  792.6 4.6 gather_fusion.3
  797.2 3.7 fusion.56
  800.9 3.7 scatter_fusion.3
  805.4 4.6 gather_fusion.3
  810.0 3.7 fusion.56
  813.7 3.7 scatter_fusion.3
  818.1 4.6 gather_fusion.3
  822.7 3.7 fusion.56
  826.4 3.7 scatter_fusion.3
  831.3 55.9 %all-reduce.6.cloned.1.call-done = f32[32,64,128]{2,1,0:T(8,128)} async-done(((f32[32,64,128]{2,1,0:T(8,128)}), f32[32,64,128]{2,1,0:T(8,128)}) %all-reduce.6.cloned.1.call-update) | async-done | bytes 1048592 | tf_op jit(solution)/shard_map/psum | solution.py:91
  891.2 106.1 %while.59 = (s32[]{:T(128)}, f32[32,256,128]{2,1,0:T(8,128)}, s32[]{:T(128)}, s32[]{:T(128)}, s32[320]{0:T(512)S(1)}, /*index=5*/bf16[320,64,256]{2,1,0:T(8,128)...) while((s32[]{:T(128)}, f32[32,256,128]{2,1,0:T(8,128)}, ...), condition=%wide.region_24.25_spmd.clone, body=%wide.region_22.24_spmd.clone.sunk | while | flops 270534016 | bytes 38803376 | solution.py:49
  892.7 6.1 fusion.59
  898.8 18.9 %scatter_fusion.4 = f32[32,256,128]{2,1,0:T(8,128)} fusion(f32[32,256,128]{2,1,0:T(8,128)} %get-tuple-element.865, s32[64]{0:T(128)S(1)} %get-tuple-element.706, f32[64,256,128]{2,1,0:T(8,128)} %fusion.59), kind=kCustom, calls=%fused_computation.9.clone.clone.1 | custom fusion | flops 2097152 | bytes 25166080 | tf_op jit(solution)/shard_map/while/body/scatter-add | solution.py:46
  919.2 6.1 fusion.59
  925.3 18.8 %scatter_fusion.4 = f32[32,256,128]{2,1,0:T(8,128)} fusion(f32[32,256,128]{2,1,0:T(8,128)} %get-tuple-element.865, s32[64]{0:T(128)S(1)} %get-tuple-element.706, f32[64,256,128]{2,1,0:T(8,128)} %fusion.59), kind=kCustom, calls=%fused_computation.9.clone.clone.1 | custom fusion | flops 2097152 | bytes 25166080 | tf_op jit(solution)/shard_map/while/body/scatter-add | solution.py:46
  945.6 6.1 fusion.59
  951.7 18.8 %scatter_fusion.4 = f32[32,256,128]{2,1,0:T(8,128)} fusion(f32[32,256,128]{2,1,0:T(8,128)} %get-tuple-element.865, s32[64]{0:T(128)S(1)} %get-tuple-element.706, f32[64,256,128]{2,1,0:T(8,128)} %fusion.59), kind=kCustom, calls=%fused_computation.9.clone.clone.1 | custom fusion | flops 2097152 | bytes 25166080 | tf_op jit(solution)/shard_map/while/body/scatter-add | solution.py:46
  972.0 6.1 fusion.59
  978.1 19.2 %scatter_fusion.4 = f32[32,256,128]{2,1,0:T(8,128)} fusion(f32[32,256,128]{2,1,0:T(8,128)} %get-tuple-element.865, s32[64]{0:T(128)S(1)} %get-tuple-element.706, f32[64,256,128]{2,1,0:T(8,128)} %fusion.59), kind=kCustom, calls=%fused_computation.9.clone.clone.1 | custom fusion | flops 2097152 | bytes 25166080 | tf_op jit(solution)/shard_map/while/body/scatter-add | solution.py:46
  997.3 110.0 %reduce-scatter.8.cloned.1.call-done = f32[1,256,128]{2,1,0:T(8,128)} async-done(((f32[32,256,128]{2,1,0:T(8,128)}), f32[1,256,128]{2,1,0:T(8,128)}) %reduce-scatter.8.cloned.1.call-update) | async-done | bytes 131088 | tf_op jit(solution)/shard_map/reduce_scatter | solution.py:63
  1108.4 65.9 %psum.47 = f32[128]{0:T(128)S(1)} all-reduce(f32[128]{0:T(128)S(1)} %multiply_reduce_fusion), channel_id=1, replica_groups=mesh['orbit'=32,'region'=4] {'orbit','region'}, use_global_device_ids=true, to_apply=%region_27.28 | all-reduce | flops 128 | bytes 1024 | tf_op jit(solution)/shard_map/psum | solution.py:66
  (98 shorter events, 44.0 us)
Async XLA Ops:
  7.2 4.8 copy-start.6
  7.2 4.8 copy-start.5
  7.2 221.7 %reduce-scatter.4.cloned.1.call-start = ((), (), s32[]{:S(2)}) async-start(), calls=%async_computation.3 | async-start | bytes 4325376 | tf_op jit(solution)/shard_map/reduce_scatter | solution.py:63
  118.0 110.8 %copy-start.7 = (f32[1,1,256]{2,1,0:T(1,128)S(1)}, f32[1,1,256]{2,1,0:T(1,128)}, u32[]{:S(2)}) copy-start(f32[1,1,256]{2,1,0:T(1,128)} %param.23) | copy-start | bytes 3076
  118.0 158.8 %all-gather.3.cloned.1.call-start = ((), (), s32[]{:S(2)}) async-start(), calls=%async_computation.4 | async-start | bytes 2162688 | tf_op jit(solution)/shard_map/all_gather | solution.py:88
  230.5 154.6 %all-reduce.4.cloned.1.call-start = ((), (), s32[]{:S(2)}) async-start(), calls=%async_computation.5 | async-start | bytes 2097152 | tf_op jit(solution)/shard_map/psum | solution.py:91
  276.9 108.2 %copy-start.4 = (f32[32,64]{1,0:T(8,128)S(1)}, f32[32,64]{1,0:T(8,128)}, u32[]{:S(2)}) copy-start(f32[32,64]{1,0:T(8,128)} %param.22) | copy-start | bytes 24580
  328.0 1.0 copy-start
  329.0 276.2 %reduce-scatter.6.cloned.1.call-start = ((), (), s32[]{:S(2)}) async-start(), calls=%async_computation.6 | async-start | bytes 4325376 | tf_op jit(solution)/shard_map/reduce_scatter | solution.py:63
  495.2 110.1 %copy-start.2 = (f32[1,256,128]{2,1,0:T(8,128)S(1)}, f32[1,256,128]{2,1,0:T(8,128)}, u32[]{:S(2)}) copy-start(f32[1,256,128]{2,1,0:T(8,128)} %reduce-scatter.4.cloned.1.call-done) | copy-start | bytes 393220
  495.2 283.8 %all-gather.5.cloned.1.call-start = ((), (), s32[]{:S(2)}) async-start(), calls=%async_computation.7 | async-start | bytes 2162688 | tf_op jit(solution)/shard_map/all_gather | solution.py:88
  737.6 149.6 %all-reduce.6.cloned.1.call-start = ((), (), s32[]{:S(2)}) async-start(), calls=%async_computation.8 | async-start | bytes 2097152 | tf_op jit(solution)/shard_map/psum | solution.py:91
  830.2 1.0 copy-start.1
  831.2 276.1 %reduce-scatter.8.cloned.1.call-start = ((), (), s32[]{:S(2)}) async-start(), calls=%async_computation.9 | async-start | bytes 4325376 | tf_op jit(solution)/shard_map/reduce_scatter | solution.py:63
  997.3 110.0 %copy-start.3 = (f32[1,256,128]{2,1,0:T(8,128)S(1)}, f32[1,256,128]{2,1,0:T(8,128)}, u32[]{:S(2)}) copy-start(f32[1,256,128]{2,1,0:T(8,128)} %reduce-scatter.6.cloned.1.call-done) | copy-start | bytes 393220
Sparse Core Ops, SparseCore 0:
  118.1 110.6 reduce-scatter.3
  231.7 45.0 all-gather.2
  329.2 55.8 all-reduce.3
  495.3 109.8 reduce-scatter.5
  737.7 41.2 all-gather.4
  831.3 55.8 all-reduce.5
  997.4 109.8 reduce-scatter.7
where the time goes:
time: 1180 us
  waiting for transfers between devices  530 us (45%)
  other arithmetic  284 us (24%)
  blocking collectives  195 us (17%)
  matrix products  103 us (9%)
  local copies, waits for them, and re-layouts  55.5 us (5%)
  between operations  14.9 us (1%)
    reduce_scatter x3, waiting for transfers between devices, reduce_tiles(): lax.psum_scatter(partial_value, 'orbit', scatter_dimension=0, tiled=True)  331 us
    scatter-add x12, other arithmetic, turn(): jax.ops.segment_sum(contrib, targets, num_segments=tile_count)  227 us
    psum x3, blocking collectives, inner_sum(): lax.psum(jnp.sum(first_vec * second_vec, axis=(0, 1)), ('orbit', 'region'))  195 us
    psum x2, waiting for transfers between devices, per_device(): image = lax.psum(partial_value, 'region')  112 us
    all_gather x2, waiting for transfers between devices, per_device(): lax.all_gather(scaled, 'orbit', axis=0, tiled=True)  87.6 us
    dot_general x12, matrix products, turn(): jnp.einsum('bsc,bsr->bcr', blocks_now, weighted[sound_ids], preferred_ele...  73.4 us
    gather x8, local copies, waits for them, and re-layouts, turn(): whole[tile_ids]  36.8 us
    scatter-add x8, other arithmetic, turn(): jax.ops.segment_sum(products, targets, num_segments=sb_count)  29.7 us
  transfers between devices with their start and end apart: 7, of which 7 were waited for; matrix products, arithmetic and copies ran while one was open for 0% of the time, Pallas kernels for 0%

commit v1 on v0

v1 whole, which is shorter than its diff:
```python
import functools
import jax
import jax.numpy as jnp
from jax import lax
from jax.experimental import pallas as pl
from jax.experimental.pallas import tpu as pltpu
from jax.sharding import PartitionSpec as P
NB=320; NSLOT=512; GMAX=128; UN=4; RING=16

def prep_kernel(cnt, bt_row, bt_col, bs_col, slots_ref, grp_ref):
    f32=jnp.float32
    n=cnt[0]
    iota=lambda shape,d: lax.broadcasted_iota(jnp.int32, shape, d)
    trow=jnp.where(iota((1,NB),1)<n, bt_row[...], 32)
    live=iota((NB,1),0)<n
    tcol=jnp.where(live, bt_col[...], 32)
    same=(trow==tcol)&(iota((NB,NB),1)<iota((NB,NB),0))
    rank=jnp.sum(jnp.where(same,1.0,0.0),axis=1,keepdims=True)
    lane=iota((NB,128),1)
    num=jnp.sum(jnp.where((tcol==lane)&(lane<32),1.0,0.0),axis=0,keepdims=True)
    g=jnp.floor((num+3.0)*0.25)
    start=jnp.sum(jnp.where(lane<tcol,jnp.broadcast_to(g,(NB,128)),0.0),axis=1,keepdims=True)
    pos=jnp.where(live,4.0*start+rank,-1.0).astype(jnp.int32)
    ident=(iota((NB,1),0)*64+bs_col[...]+1).astype(f32)
    hit=pos==iota((NB,NSLOT),1)
    slots_ref[...]=jnp.sum(jnp.where(hit,jnp.broadcast_to(ident,(NB,NSLOT)),0.0),axis=0,keepdims=True).astype(jnp.int32)
    l2=iota((128,128),1); s2=iota((128,128),0)
    gend=jnp.sum(jnp.where(l2<=s2,jnp.broadcast_to(g,(128,128)),0.0),axis=1,keepdims=True)
    gt=jnp.sum(jnp.where((s2<32)&(gend<=l2.astype(f32)),1.0,0.0),axis=0,keepdims=True)
    total=jnp.sum(g,axis=1,keepdims=True)
    grp_ref[...]=jnp.where(iota((1,128),1)==127,jnp.broadcast_to(total,(1,128)),gt).astype(jnp.int32)

def prep(count, bs, bt):
    return pl.pallas_call(prep_kernel,
        out_shape=(jax.ShapeDtypeStruct((1,NSLOT),jnp.int32),jax.ShapeDtypeStruct((1,128),jnp.int32)),
        in_specs=[pl.BlockSpec(memory_space=pltpu.SMEM)]+[pl.BlockSpec(memory_space=pltpu.VMEM)]*3,
        out_specs=(pl.BlockSpec(memory_space=pltpu.VMEM),)*2,
        name="prep",
    )(count, bt.reshape(1,NB), bt.reshape(NB,1), bs.reshape(NB,1))

NCH=8
def group_loop(slots, grp, F, buf, sem, body, before):
    for k in range(NCH):
        pltpu.make_async_copy(F.at[pl.ds(k*NB//NCH,NB//NCH)], buf.at[pl.ds(k*NB//NCH,NB//NCH)], sem.at[k]).start()
    before()
    for k in range(NCH):
        pltpu.make_async_copy(F.at[pl.ds(k*NB//NCH,NB//NCH)], buf.at[pl.ds(k*NB//NCH,NB//NCH)], sem.at[k]).wait()
    turns=lax.shift_right_logical(grp[0,127]+(UN-1),2)
    def turn(i,c):
        body(i)
        return c
    lax.fori_loop(0,turns,turn,0)

def rows(slots,buf,g):
    out=[]
    for k in range(4):
        v=slots[0,4*g+k]
        out.append(buf[lax.shift_right_logical(jnp.maximum(v-1,0),6)])
    return jnp.concatenate(out,axis=0)

def snd(slots,g,k):
    v=slots[0,4*g+k]
    return jnp.where(v==0,32,jnp.bitwise_and(v-1,63))

def t_kernel(slots, grp, F, w, pa, pb, acc, wt0, wt1, buf, sem):
    def before():
        lane=lax.broadcasted_iota(jnp.int32,(128,128),1)
        for p in range(16):
            x=jnp.concatenate([w[2*p],w[2*p+1]],axis=0).astype(jnp.float32).T
            y=pltpu.roll(x,64,1)
            lo=lane<64
            z=jnp.zeros_like(x)
            wt0[2*p]=jnp.where(lo,x,z).astype(jnp.bfloat16)
            wt1[2*p]=jnp.where(lo,z,y).astype(jnp.bfloat16)
            wt0[2*p+1]=jnp.where(lo,y,z).astype(jnp.bfloat16)
            wt1[2*p+1]=jnp.where(lo,z,x).astype(jnp.bfloat16)
        wt0[32]=jnp.zeros((128,128),jnp.bfloat16)
        wt1[32]=jnp.zeros((128,128),jnp.bfloat16)
        acc[...]=jnp.zeros_like(acc)
    def body(i):
        outs=[]
        for j in range(UN):
            g=i*UN+j
            s=[snd(slots,g,k) for k in range(4)]
            lhs=jnp.concatenate([wt0[s[0]]+wt1[s[1]],wt0[s[2]]+wt1[s[3]]],axis=1)
            outs.append(jnp.dot(lhs,rows(slots,buf,g),preferred_element_type=jnp.float32))
        for j in range(UN):
            t=grp[0,i*UN+j]
            acc[t]+=outs[j]
    group_loop(slots,grp,F,buf,sem,body,before)
    for y in range(4):
        for z in range(4):
            for c in range(2):
                x=acc[(y*4+z)*2+c].astype(pa.dtype)
                pa[c,y,z]=x[0:64]
                pb[c,z,y]=x[64:128]

SM=pl.BlockSpec(memory_space=pltpu.SMEM); VM=pl.BlockSpec(memory_space=pltpu.VMEM); AN=pl.BlockSpec(memory_space=pl.ANY)
def transpose_map(slots, grp, F, w, dtype):
    o=jax.ShapeDtypeStruct((2,4,4,64,256),dtype)
    return pl.pallas_call(t_kernel,out_shape=(o,o),in_specs=[SM,SM,AN,VM],out_specs=(VM,VM),
        scratch_shapes=[pltpu.VMEM((33,128,256),jnp.float32),pltpu.VMEM((33,128,128),jnp.bfloat16),pltpu.VMEM((33,128,128),jnp.bfloat16),
            pltpu.VMEM((NB,64,256),jnp.bfloat16),pltpu.SemaphoreType.DMA((NCH,))],
        compiler_params=pltpu.CompilerParams(vmem_limit_bytes=32<<20), name="tmap")(slots,grp,F,w)

def f_kernel(slots, grp, F, va, vb, img, acc, buf, sem):
    def before():
        acc[...]=jnp.zeros_like(acc)
    def body(i):
        outs=[]
        for j in range(UN):
            g=i*UN+j
            t=jnp.minimum(grp[0,g],31)
            c=jnp.bitwise_and(t,1); yz=lax.shift_right_logical(t,1)
            zy=jnp.bitwise_and(yz,3)*4+lax.shift_right_logical(yz,2)
            rhs=jnp.concatenate([va[c,yz],vb[c,zy]],axis=0)
            outs.append(jnp.dot(rows(slots,buf,g),rhs,preferred_element_type=jnp.float32))
        for j in range(UN):
            for k in range(4):
                s=snd(slots,i*UN+j,k)
                acc[s]+=outs[j][64*k:64*k+64]
    group_loop(slots,grp,F,buf,sem,body,before)
    img[...]=acc[0:32].astype(img.dtype)

def forward_map(slots, grp, F, va, vb, dtype):
    return pl.pallas_call(f_kernel,out_shape=jax.ShapeDtypeStruct((32,64,128),dtype),in_specs=[SM,SM,AN,VM,VM],out_specs=VM,
        scratch_shapes=[pltpu.VMEM((33,64,128),jnp.float32),pltpu.VMEM((NB,64,256),jnp.bfloat16),pltpu.SemaphoreType.DMA((NCH,))],
        compiler_params=pltpu.CompilerParams(vmem_limit_bytes=32<<20), name="fmap")(slots,grp,F,va.reshape(2,16,128,128),vb.reshape(2,16,128,128))
MESH=pl.DeviceIdType.MESH
f32=jnp.float32; bf16=jnp.bfloat16

class Net:
    def __init__(self, send, recv):
        self.send, self.recv, self.n = send, recv, 0
    def put(self, src, dst, dev):
        k=self.n; self.n+=1
        c=pltpu.make_async_remote_copy(src_ref=src,dst_ref=dst,send_sem=self.send.at[k],recv_sem=self.recv.at[k],device_id=dev,device_id_type=MESH)
        c.start()
        return c

def place():
    o=lax.axis_index("orbit"); r=lax.axis_index("region")
    y=o//8; z=(o//2)%4; c=o%2
    return y,z,c,r
def dev(y,z,c,r): return (y*8+z*2+c, r)

def greet(devs):
    bar=pltpu.get_barrier_semaphore()
    for d in devs:
        pl.semaphore_signal(bar,inc=1,device_id=d,device_id_type=MESH)
    pl.semaphore_wait(bar,len(devs))

class Ring:
    def __init__(self, i, at):
        self.i=i; self.right=(i+1)%4; self.left=(i+3)%4; self.opp=(i+2)%4
        self.dr=at(self.right); self.dl=at(self.left)
        self.b1=at(i+1-2*(i%2)); self.b2=at(3-i)

def rs_begin(net, ring, q, ri, gr, gl):
    h=q.shape[1]//2
    ra=net.put(q.at[ring.opp,pl.ds(0,h)], ri.at[0], ring.dr)
    la=net.put(q.at[ring.opp,pl.ds(h,h)], ri.at[1], ring.dl)
    rb=net.put(q.at[ring.right,pl.ds(h,h)], gr.at[pl.ds(h,h)], ring.dr)
    lb=net.put(q.at[ring.left,pl.ds(0,h)], gl.at[pl.ds(0,h)], ring.dl)
    return [ra,la,rb,lb]
def rs_relay(net, ring, q, ri, so, gr, gl, cs):
    h=q.shape[1]//2
    cs[0].wait_recv()
    so[0]=(q[ring.right,pl.ds(0,h)].astype(f32)+ri[0].astype(f32)).astype(so.dtype)
    cs.append(net.put(so.at[0], gr.at[pl.ds(0,h)], ring.dr))
    cs[1].wait_recv()
    so[1]=(q[ring.left,pl.ds(h,h)].astype(f32)+ri[1].astype(f32)).astype(so.dtype)
    cs.append(net.put(so.at[1], gl.at[pl.ds(h,h)], ring.dl))
def rs_end(cs):
    for c in cs[2:]: c.wait_recv()
def drain(cs):
    for c in cs: c.wait_send()

def ag_begin(net, ring, x):
    s=x.at[ring.i]
    return [net.put(s,s,ring.dr), net.put(s,s,ring.dl)]
def ag_relay(net, ring, x, cs):
    h=x.shape[1]//2
    cs[0].wait_recv()
    s=x.at[ring.left,pl.ds(0,h)]
    cs.append(net.put(s,s,ring.dr))
    cs[1].wait_recv()
    s=x.at[ring.right,pl.ds(h,h)]
    cs.append(net.put(s,s,ring.dl))
def ag_end(cs):
    cs[2].wait_recv(); cs[3].wait_recv()

def hop(net, sin, sout, k, d):
    return net.put(sout.at[k], sin.at[k], d)

def rs_scratch(dt, cdt):
    V=pltpu.VMEM
    out=[V((4,4,64,256),cdt)]*2
    out+=[V((4,4,64,256),dt)]*2
    out+=[V((2,2,64,256),dt),V((2,2,64,256),dt),V((4,64,256),dt),V((4,64,256),dt)]*2
    out+=[V((4,64,256),dt)]*2
    out+=[V((2,32,256),dt),V((2,32,256),dt),V((64,256),dt),V((64,256),dt)]*2
    return out

def reduce_tiles(net, pos, ry, rz, pa, pb, sc, tick=lambda k:None):
    y,z,c,r=pos
    ra,rb,qa,qb=sc[0:4]; a1=sc[4:8]; b1=sc[8:12]; sa,sb=sc[12:14]; a2=sc[14:18]; b2=sc[18:22]
    mate=dev(y,z,1-c,r)
    ks=[]
    oy=[ry.opp,ry.right,ry.left,ry.i]; oz=[rz.opp,rz.right,rz.left,rz.i]
    for k in range(4):
        ks.append((net.put(pa.at[1-c,oy[k]],ra.at[oy[k]],mate), net.put(pb.at[1-c,oz[k]],rb.at[oz[k]],mate)))
    tick(0)
    for k in range(4):
        ks[k][0].wait_recv()
        qa[oy[k]]=(pa[c,oy[k]].astype(f32)+ra[oy[k]].astype(f32)).astype(qa.dtype)
        ks[k][1].wait_recv()
        qb[oz[k]]=(pb[c,oz[k]].astype(f32)+rb[oz[k]].astype(f32)).astype(qb.dtype)
        if k==2:
            ca=rs_begin(net,ry,qa,a1[0],a1[2],a1[3])
            cb=rs_begin(net,rz,qb,b1[0],b1[2],b1[3])
    tick(1)
    rs_relay(net,ry,qa,*a1,ca); rs_relay(net,rz,qb,*b1,cb)
    tick(2)
    rs_end(ca)
    sa[...]=(qa[ry.i].astype(f32)+a1[2][...].astype(f32)+a1[3][...].astype(f32)).astype(sa.dtype)
    da=rs_begin(net,rz,sa,a2[0],a2[2],a2[3])
    rs_end(cb)
    sb[...]=(qb[rz.i].astype(f32)+b1[2][...].astype(f32)+b1[3][...].astype(f32)).astype(sb.dtype)
    db=rs_begin(net,ry,sb,b2[0],b2[2],b2[3])
    tick(3)
    rs_relay(net,rz,sa,*a2,da); rs_relay(net,ry,sb,*b2,db)
    tick(4)
    own_a=qa[ry.i,rz.i].astype(f32)+a1[2][rz.i].astype(f32)+a1[3][rz.i].astype(f32)
    rs_end(da)
    own_a=own_a+a2[2][...].astype(f32)+a2[3][...].astype(f32)
    own_b=qb[rz.i,ry.i].astype(f32)+b1[2][ry.i].astype(f32)+b1[3][ry.i].astype(f32)
    rs_end(db)
    own_b=own_b+b2[2][...].astype(f32)+b2[3][...].astype(f32)
    flat=[x for p in ks for x in p]+ca+cb+da+db
    return jnp.concatenate([own_a,own_b],axis=0), flat

def gather_tiles(net, pos, ry, rz, va, vb, tick=lambda k:None):
    y,z,c,r=pos
    mate=dev(y,z,1-c,r)
    a=ag_begin(net,rz,va.at[c,ry.i]); b=ag_begin(net,ry,vb.at[c,rz.i])
    tick(0)
    ag_relay(net,rz,va.at[c,ry.i],a); ag_relay(net,ry,vb.at[c,rz.i],b)
    tick(1)
    ag_end(a); a2=ag_begin(net,ry,va.at[c])
    ag_end(b); b2=ag_begin(net,rz,vb.at[c])
    ks=[]
    def across(v,i):
        s=v.at[c,i]
        ks.append(net.put(s,s,mate))
    across(va,ry.i); across(vb,rz.i)
    tick(2)
    ag_relay(net,ry,va.at[c],a2); ag_relay(net,rz,vb.at[c],b2)
    across(va,ry.left); across(va,ry.right); across(vb,rz.left); across(vb,rz.right)
    tick(3)
    ag_end(a2); across(va,ry.opp)
    ag_end(b2); across(vb,rz.opp)
    for k in ks: k.wait_recv()
    return a+b+a2+b2+ks

class Reduce:
    def __init__(self, net, sin, sout, hops, base=0):
        self.net, self.sin, self.sout, self.hops, self.base = net, sin, sout, hops, base
        self.k=0; self.cs=[]
    def start(self, value):
        self.value=value
        self._send()
    def _send(self):
        j=self.base+self.k
        self.sout[j]=self.value
        self.cs.append(self.net.put(self.sout.at[j], self.sin.at[j], self.hops[self.k]))
    def step(self):
        j=self.base+self.k
        self.cs[self.k].wait_recv()
        self.value=self.value+self.sin[j]
        self.k+=1
        if self.k<len(self.hops): self._send()
    def finish(self):
        while self.k<len(self.hops): self.step()
        return self.value

def rep(v):
    return jnp.broadcast_to(v,(8,128))
NS=96

def first_kernel(pa, pb, prior, r0, va, vb, npl, *s):
    sc=s[:22]; sin,sout,ssem,rsem=s[22:]
    pos=y,z,c,r=place()
    ry=Ring(y,lambda i:dev(i,z,c,r)); rz=Ring(z,lambda i:dev(y,i,c,r))
    greet([dev(y,z,1-c,r),ry.dr,ry.dl,rz.dr,rz.dl])
    net=Net(ssem,rsem)
    t,cs=reduce_tiles(net,pos,ry,rz,pa,pb,sc)
    res=prior[...]*t.T
    r0[...]=res
    v=(prior[...]*res).astype(bf16)
    va[c,y,z]=v[0:128]; vb[c,z,y]=v[128:256]
    red=Reduce(net,sin,sout,[dev(y,z,1-c,r),ry.b1,ry.b2,rz.b1,rz.b2])
    def tick(k):
        if k==0: red.start(rep(jnp.sum(res*res,axis=0,keepdims=True)))
        else: red.step()
    cs2=gather_tiles(net,pos,ry,rz,va,vb,tick)
    npl[...]=red.finish()
    drain(cs+cs2+red.cs)

def mid_kernel(pa, pb, prior, r0, nrm, wi, r1, d1, it, nn, va, vb, dd, *s):
    sc=s[:22]; sin,sout,ssem,rsem=s[22:]
    pos=y,z,c,r=place()
    ry=Ring(y,lambda i:dev(i,z,c,r)); rz=Ring(z,lambda i:dev(y,i,c,r)); rx=Ring(r,lambda i:dev(y,z,c,i))
    greet([dev(y,z,1-c,r),ry.dr,ry.dl,rz.dr,rz.dl,rx.dr,rx.dl])
    net=Net(ssem,rsem)
    plane=[dev(y,z,1-c,r),ry.b1,ry.b2,rz.b1,rz.b2]
    ra=Reduce(net,sin,sout,plane,0)
    def tick(k):
        if k==0: ra.start(wi[...])
        else: ra.step()
    t,cs=reduce_tiles(net,pos,ry,rz,pa,pb,sc,tick)
    n0=nrm[0:1]
    step=n0/(n0+ra.finish()[0:1])
    d0=r0[...]
    p=d0+prior[...]*t.T
    res=d0-step*p
    rb=Reduce(net,sin,sout,plane+[rx.b1,rx.b2],5)
    rb.start(rep(jnp.sum(res*res,axis=0,keepdims=True)))
    it[...]=step*d0
    r1[...]=res
    n1=rb.finish()
    nn[...]=n1
    d=res+(n1[0:1]/n0)*d0
    d1[...]=d
    v=(prior[...]*d).astype(bf16)
    va[c,y,z]=v[0:128]; vb[c,z,y]=v[128:256]
    rc=Reduce(net,sin,sout,plane,12)
    def tick2(k):
        if k==0: rc.start(rep(jnp.sum(d*d,axis=0,keepdims=True)))
        else: rc.step()
    cs2=gather_tiles(net,pos,ry,rz,va,vb,tick2)
    dd[...]=rc.finish()
    drain(cs+cs2+ra.cs+rb.cs+rc.cs)

def last_kernel(pa, pb, prior, r1, d1, it, n1, dd, wi, flux, resid, *s):
    sc=s[:22]; sin,sout,ssem,rsem=s[22:]
    pos=y,z,c,r=place()
    ry=Ring(y,lambda i:dev(i,z,c,r)); rz=Ring(z,lambda i:dev(y,i,c,r))
    greet([dev(y,z,1-c,r),ry.dr,ry.dl,rz.dr,rz.dl])
    net=Net(ssem,rsem)
    ra=Reduce(net,sin,sout,[dev(y,z,1-c,r),ry.b1,ry.b2,rz.b1,rz.b2],0)
    def tick(k):
        if k==0: ra.start(wi[...])
        else: ra.step()
    t,cs=reduce_tiles(net,pos,ry,rz,pa,pb,sc,tick)
    step=n1[0:1]/(dd[0:1]+ra.finish()[0:1])
    p=d1[...]+prior[...]*t.T
    resid[...]=r1[...]-step*p
    flux[...]=prior[...]*(it[...]+step*d1[...])
    drain(cs+ra.cs)

def cross_kernel(img, wgt, part, w, tot, wi, ri, so, gr, gl, sin, sout, ssem, rsem):
    pos=y,z,c,r=place()
    rx=Ring(r,lambda i:dev(y,z,c,i))
    greet([rx.dr,rx.dl])
    net=Net(ssem,rsem)
    cs=rs_begin(net,rx,img,ri,gr,gl)
    ra=Reduce(net,sin,sout,[rx.b1,rx.b2],0)
    ra.start(part[...])
    rs_relay(net,rx,img,ri,so,gr,gl,cs)
    ra.step()
    rs_end(cs)
    total=img[r].astype(f32)+gr[...].astype(f32)+gl[...].astype(f32)
    wt=wgt[...]
    scaled=wt*total
    w[r]=scaled.astype(bf16)
    ag=ag_begin(net,rx,w)
    rb=Reduce(net,sin,sout,[rx.b1,rx.b2],2)
    rb.start(rep(jnp.sum(jnp.sum(scaled*total,axis=0),axis=0,keepdims=True)))
    ag_relay(net,rx,w,ag)
    rb.step()
    tot[...]=ra.finish()
    wi[...]=rb.finish()
    ag_end(ag)
    drain(cs+ag+ra.cs+rb.cs)

VM=pl.BlockSpec(memory_space=pltpu.VMEM)
def _call(kernel, outs, scratch, cid, name, *args):
    return pl.pallas_call(kernel,out_shape=outs,in_specs=[VM]*len(args),out_specs=tuple([VM]*len(outs)),
        scratch_shapes=scratch,compiler_params=pltpu.CompilerParams(collective_id=cid,has_side_effects=True,vmem_limit_bytes=40<<20),name=name)(*args)
SH=lambda shape,dt=f32: jax.ShapeDtypeStruct(shape,dt)
VA=SH((2,4,4,128,128),bf16); ROW=SH((8,128)); TILE=SH((256,128))
def tail(n): return [pltpu.VMEM((n,8,128),f32)]*2+[pltpu.SemaphoreType.DMA((NS,))]*2
def first(pa,pb,prior):
    return _call(first_kernel,[TILE,VA,VA,ROW],rs_scratch(f32,f32)+tail(5),0,"first",pa,pb,prior)
def mid(pa,pb,prior,r0,nrm,wi):
    return _call(mid_kernel,[TILE,TILE,TILE,ROW,VA,VA,ROW],rs_scratch(bf16,pa.dtype)+tail(17),1,"mid",pa,pb,prior,r0,nrm,wi)
def last(pa,pb,prior,r1,d1,it,n1,dd,wi):
    return _call(last_kernel,[TILE,TILE],rs_scratch(bf16,pa.dtype)+tail(5),2,"last",pa,pb,prior,r1,d1,it,n1,dd,wi)
def cross(img,wgt,part):
    V=pltpu.VMEM
    return _call(cross_kernel,[SH((4,8,64,128),bf16),ROW,ROW],[V((2,4,64,128),bf16)]*2+[V((8,64,128),bf16)]*2+tail(4),3,"cross",img.reshape(4,8,64,128),wgt,part)

def per_device(footprints, block_sounding, block_tile, block_count, observations, obs_weight, prior_std):
    slots, grp = prep(block_count, block_sounding, block_tile)
    w0 = (obs_weight[:, :, None] * observations).astype(bf16)
    prior = jnp.broadcast_to(prior_std.reshape(256, 1), (256, 128))
    mine = lax.dynamic_slice_in_dim(obs_weight, 8 * lax.axis_index("region"), 8, 0)
    wgt = jnp.broadcast_to(mine[:, :, None], (8, 64, 128))
    pa, pb = transpose_map(slots, grp, footprints, w0, f32)
    r0, va, vb, norm = first(pa, pb, prior)
    img = forward_map(slots, grp, footprints, va, vb, bf16)
    w, norm, wi = cross(img, wgt, norm)
    pa, pb = transpose_map(slots, grp, footprints, w.reshape(32, 64, 128), f32)
    r1, d1, it, n1, va, vb, dd = mid(pa, pb, prior, r0, norm, wi)
    img = forward_map(slots, grp, footprints, va, vb, bf16)
    w, dd, wi = cross(img, wgt, dd)
    pa, pb = transpose_map(slots, grp, footprints, w.reshape(32, 64, 128), bf16)
    flux, resid = last(pa, pb, prior, r1, d1, it, n1, dd, wi)
    return flux[None, None], resid[None, None]


def solution(mesh):
    return jax.shard_map(
        per_device,
        mesh=mesh,
        in_specs=(
            P(("orbit", "region"), None, None),
            P(("orbit", "region")),
            P(("orbit", "region")),
            P(("orbit", "region")),
            P("orbit", None, None),
            P("orbit", None),
            P("region", "orbit", None),
        ),
        out_specs=(P("region", "orbit", None, None), P("region", "orbit", None, None)),
        check_vma=False,
    )
```

time: 1180 us -> 219 us (0.19)
  waiting for transfers between devices: 530 us -> 0 us
  other arithmetic: 284 us -> 1.57 us
  Pallas kernels: 0 us -> 202 us
  blocking collectives: 195 us -> 0 us
  matrix products: 103 us -> 0 us
  local copies, waits for them, and re-layouts: 55.5 us -> 12.3 us
  between operations: 14.9 us -> 1.43 us
    reduce_scatter x3 -> x0, waiting for transfers between devices: 331 us -> none  [reduce_tiles(): lax.psum_scatter(partial_value, 'orbit', scatter_dimension=0, tiled=True)]
    scatter-add x20 -> x0, other arithmetic: 257 us -> none  [the longest x12 227 us: turn(): jax.ops.segment_sum(contrib, targets, num_segments=tile_count)]
    pallas_call x0 -> x11, Pallas kernels: none -> 202 us  [the longest x5 162 us: _call(): pl.pallas_call(kernel, out_shape=outs, in_specs=[VM] * len(args), out_spe...]
    psum x3 -> x0, blocking collectives: 195 us -> none  [inner_sum(): lax.psum(jnp.sum(first_vec * second_vec, axis=(0, 1)), ('orbit', 'region'))]
    psum x2 -> x0, waiting for transfers between devices: 112 us -> none  [per_device(): image = lax.psum(partial_value, 'region')]
    dot_general x20 -> x0, matrix products: 103 us -> none  [the longest x12 73.4 us: turn(): jnp.einsum('bsc,bsr->bcr', blocks_now, weighted[sound_ids], preferred_ele...]
    all_gather x2 -> x0, waiting for transfers between devices: 87.6 us -> none  [per_device(): lax.all_gather(scaled, 'orbit', axis=0, tiled=True)]
    gather x20 -> x0, local copies, waits for them, and re-layouts: 45.8 us -> none  [the longest x8 36.8 us: turn(): whole[tile_ids]]
  transfers between devices with their start and end apart: 7 -> 0, of which waited for: 7 -> 0; matrix products, arithmetic and copies ran while one was open for 0% -> 0% of each run, Pallas kernels for 0% -> 0%
where the time goes in v1:
time: 219 us; the launch traced here: 217 us
  Pallas kernels  202 us (92%)
  local copies, waits for them, and re-layouts  12.3 us (6%)
    pallas_call x5, Pallas kernels, _call(): pl.pallas_call(kernel, out_shape=outs, in_specs=[VM] * len(args), out_spe...  162 us
    pallas_call x3, Pallas kernels, transpose_map(): pl.pallas_call(t_kernel, out_shape=(o, o), in_specs=[SM, SM, AN, VM], out...  22.5 us
    pallas_call x2, Pallas kernels, forward_map(): pl.pallas_call(f_kernel, out_shape=jax.ShapeDtypeStruct((32, 64, 128), dt...  15.2 us
    unnamed x14, local copies, waits for them, and re-layouts  6.61 us

profile of v1, /device:TPU:1, one launch (start us, length us, event | category | flops | bytes accessed | tf_op | source)
XLA Modules:
  0.0 216.9 jit_solution(6295275769364761202)
XLA Ops:
  1.3 1.2 reshape.41.bt_row
  2.5 0.7 constant_dynamic-slice_fusion
  3.2 0.8 broadcast_in_dim.21.prior
  4.0 1.5 reshape.53.bs_col
  5.4 1.5 reshape.52.bt_col
  6.9 1.9 prep.1
  8.8 0.1 broadcast_in_dim.22.wgt
  9.0 1.6 multiply_convert_fusion.w
  10.5 0.0 copy-start
  10.5 4.0 %copy-done = bf16[320,64,256]{2,1,0:T(8,128)(2,1)S(1)} copy-done((bf16[320,64,256]{2,1,0:T(8,128)(2,1)S(1)}, bf16[320,64,256]{2,1,0:T(8,128)(2,1)}, u32[]{:S(2)}) %copy-start) | copy-done | bytes 10485784
  14.5 0.0 copy-start.2
  14.5 0.7 copy-done.2
  15.2 0.0 copy-start.4
  15.2 0.6 copy-done.4
  15.8 0.0 copy-start.1
  15.8 7.5 %tmap.3 = (f32[2,4,4,64,256]{4,3,2,1,0:T(8,128)S(1)}, f32[2,4,4,64,256]{4,3,2,1,0:T(8,128)S(1)}) custom-call(s32[1,512]{1,0:T(1,128)S(1)} %copy-done.2, s32[1,128]{1,0:T(1,128)S(1)} %copy-done.4, bf16[320,64,256]{2,1,0:T(8,128)(2,1)S(1)} %copy-done, bf16[32,64,128]{2,1,0:T(8,128)(2,1)S(1)} %multiply_convert_fusion.w), custom_call_target="tpu_custom_call" | custom-call | tf_op jit(solution)/shard_map/tmap/pallas_call | solution.py:101
  23.4 0.0 copy-start.3
  23.4 0.0 copy-start.5
  23.4 48.3 %first.1 = (f32[256,128]{1,0:T(8,128)S(1)}, bf16[2,4,4,128,128]{4,3,2,1,0:T(8,128)(2,1)S(1)}, bf16[2,4,4,128,128]{4,3,2,1,0:T(8,128)(2,1)S(1)}, f32[8,128]{1,0:T(8,128)S(1)}) custom-call(f32[2,4,4,64,256]{4,3,2,1,0:T(8,128)S(1)} %get-tuple-element.31.pa, f32[2,4,4,64,256]{4,3,2,1,0:T(8,128)S(1)} %get-tuple-element.32.pb, f32[256,128]{1,0:T(8,128)S(1)} %broadcast_in_dim.21.prior), custom_call_target="tpu_custom_call" | custom-call | tf_op jit(solution)/shard_map/first/pallas_call | solution.py:389
  71.7 0.0 copy-done.1
  71.7 0.0 copy-done.3
  71.7 0.0 copy-done.5
  71.7 7.6 %fmap.2 = bf16[32,64,128]{2,1,0:T(8,128)(2,1)S(1)} custom-call(s32[1,512]{1,0:T(1,128)S(1)} %copy-done.3, s32[1,128]{1,0:T(1,128)S(1)} %copy-done.5, bf16[320,64,256]{2,1,0:T(8,128)(2,1)S(1)} %copy-done.1, bf16[2,16,128,128]{3,2,1,0:T(8,128)(2,1)S(1)} %bitcast.15, bf16[2,16,128,128]{3,2,1,0:T(8,128)(2,1)S(1)} %bitcast.16), custom_call_target="tpu_custom_call" | custom-call | tf_op jit(solution)/shard_map/fmap/pallas_call | solution.py:126
  79.4 17.9 %cross.2 = (bf16[4,8,64,128]{3,2,1,0:T(8,128)(2,1)S(1)}, f32[8,128]{1,0:T(8,128)S(1)}, f32[8,128]{1,0:T(8,128)S(1)}) custom-call(bf16[4,8,64,128]{3,2,1,0:T(8,128)(2,1)S(1)} %bitcast.12, f32[8,64,128]{2,1,0:T(8,128)S(1)} %broadcast_in_dim.22.wgt, f32[8,128]{1,0:T(8,128)S(1)} %get-tuple-element.35.part), custom_call_target="tpu_custom_call" | custom-call | tf_op jit(solution)/shard_map/cross/pallas_call | solution.py:389
  97.2 7.5 %tmap.4 = (f32[2,4,4,64,256]{4,3,2,1,0:T(8,128)S(1)}, f32[2,4,4,64,256]{4,3,2,1,0:T(8,128)S(1)}) custom-call(s32[1,512]{1,0:T(1,128)S(1)} %copy-done.3, s32[1,128]{1,0:T(1,128)S(1)} %copy-done.5, bf16[320,64,256]{2,1,0:T(8,128)(2,1)S(1)} %copy-done.1, bf16[32,64,128]{2,1,0:T(8,128)(2,1)S(1)} %bitcast.18), custom_call_target="tpu_custom_call" | custom-call | tf_op jit(solution)/shard_map/tmap/pallas_call | solution.py:101
  104.8 59.0 %mid.1 = (f32[256,128]{1,0:T(8,128)S(1)}, f32[256,128]{1,0:T(8,128)S(1)}, f32[256,128]{1,0:T(8,128)S(1)}, f32[8,128]{1,0:T(8,128)S(1)}, bf16[2,4,4,128,128]{4,3,...) custom-call(f32[2,4,4,64,256]{4,3,2,1,0:T(8,128)S(1)} %get-tuple-element.37.pa, ...), custom_call_target="tpu_custom_call" | custom-call | tf_op jit(solution)/shard_map/mid/pallas_call | solution.py:389
  163.8 7.6 %fmap.3 = bf16[32,64,128]{2,1,0:T(8,128)(2,1)S(1)} custom-call(s32[1,512]{1,0:T(1,128)S(1)} %copy-done.3, s32[1,128]{1,0:T(1,128)S(1)} %copy-done.5, bf16[320,64,256]{2,1,0:T(8,128)(2,1)S(1)} %copy-done.1, bf16[2,16,128,128]{3,2,1,0:T(8,128)(2,1)S(1)} %bitcast.13, bf16[2,16,128,128]{3,2,1,0:T(8,128)(2,1)S(1)} %bitcast.14), custom_call_target="tpu_custom_call" | custom-call | tf_op jit(solution)/shard_map/fmap/pallas_call | solution.py:126
  171.4 15.8 %cross.3 = (bf16[4,8,64,128]{3,2,1,0:T(8,128)(2,1)S(1)}, f32[8,128]{1,0:T(8,128)S(1)}, f32[8,128]{1,0:T(8,128)S(1)}) custom-call(bf16[4,8,64,128]{3,2,1,0:T(8,128)(2,1)S(1)} %bitcast.11, f32[8,64,128]{2,1,0:T(8,128)S(1)} %broadcast_in_dim.22.wgt, f32[8,128]{1,0:T(8,128)S(1)} %get-tuple-element.44.part), custom_call_target="tpu_custom_call" | custom-call | tf_op jit(solution)/shard_map/cross/pallas_call | solution.py:389
  187.2 7.5 %tmap.5 = (bf16[2,4,4,64,256]{4,3,2,1,0:T(8,128)(2,1)S(1)}, bf16[2,4,4,64,256]{4,3,2,1,0:T(8,128)(2,1)S(1)}) custom-call(s32[1,512]{1,0:T(1,128)S(1)} %copy-done.3, s32[1,128]{1,0:T(1,128)S(1)} %copy-done.5, bf16[320,64,256]{2,1,0:T(8,128)(2,1)S(1)} %copy-done.1, bf16[32,64,128]{2,1,0:T(8,128)(2,1)S(1)} %bitcast.17), custom_call_target="tpu_custom_call" | custom-call | tf_op jit(solution)/shard_map/tmap/pallas_call | solution.py:101
  194.7 20.9 %last.1 = (f32[256,128]{1,0:T(8,128)S(1)}, f32[256,128]{1,0:T(8,128)S(1)}) custom-call(bf16[2,4,4,64,256]{4,3,2,1,0:T(8,128)(2,1)S(1)} %get-tuple-element.46.pa, bf16[2,4,4,64,256]{4,3,2,1,0:T(8,128)(2,1)S(1)} %get-tuple-element.47.pb, f32[256,128]{1,0:T(8,128)S(1)} %broadcast_in_dim.21.prior, f32[256,128]{1,0:T(8,128)S(1)} %get-tuple-element.48.r1, ...), custom_call_target="tpu_custom_call" | custom-call | tf_op jit(solution)/shard_map/last/pallas_call | solution.py:389
  215.6 0.7 copy.14
  216.2 0.7 copy.15
Async XLA Ops:
  10.5 4.0 %copy-start = (bf16[320,64,256]{2,1,0:T(8,128)(2,1)S(1)}, bf16[320,64,256]{2,1,0:T(8,128)(2,1)}, u32[]{:S(2)}) copy-start(bf16[320,64,256]{2,1,0:T(8,128)(2,1)} %F.9) | copy-start | bytes 31457284
  14.5 0.7 copy-start.2
  15.2 0.6 copy-start.4
  15.8 55.9 %copy-start.1 = (bf16[320,64,256]{2,1,0:T(8,128)(2,1)S(1)}, bf16[320,64,256]{2,1,0:T(8,128)(2,1)}, u32[]{:S(2)}) copy-start(bf16[320,64,256]{2,1,0:T(8,128)(2,1)} %F.9) | copy-start | bytes 31457284
  23.4 48.4 %copy-start.3 = (s32[1,512]{1,0:T(1,128)S(1)}, s32[1,512]{1,0:T(1,128)}, u32[]{:S(2)}) copy-start(s32[1,512]{1,0:T(1,128)} %get-tuple-element.29.slots) | copy-start | bytes 6148
  23.4 48.4 %copy-start.5 = (s32[1,128]{1,0:T(1,128)S(1)}, s32[1,128]{1,0:T(1,128)}, u32[]{:S(2)}) copy-start(s32[1,128]{1,0:T(1,128)} %get-tuple-element.30.grp) | copy-start | bytes 1540

commit v2 on v0

v2 whole, which is shorter than its diff:
```python
import jax
import jax.numpy as jnp
from jax import lax
from jax.experimental import pallas as pl
from jax.experimental.pallas import tpu as pltpu
from jax.sharding import PartitionSpec as P

f32 = jnp.float32
bf16 = jnp.bfloat16
def SH(shape, dtype=f32): return jax.ShapeDtypeStruct(shape, dtype)

NB=320; NBP=384; NSLOT=512; UN=16; NCH=4

def sort_blocks(n, bt_row, bt_col, bs_col):
    iota=lambda shape,d: lax.broadcasted_iota(jnp.int32, shape, d)
    trow=jnp.where(iota((1,NBP),1)<n, bt_row, 32.0)
    live=iota((NBP,1),0)<n
    tcol=jnp.where(live, bt_col, 32.0)
    same=(trow==tcol)&(iota((NBP,NBP),1)<iota((NBP,NBP),0))
    rank=jnp.sum(jnp.where(same,1.0,0.0),axis=1,keepdims=True)
    lane=iota((NBP,128),1); lanef=lane.astype(f32)
    num=jnp.sum(jnp.where((tcol==lanef)&(lane<32),1.0,0.0),axis=0,keepdims=True)
    g=jnp.floor((num+3.0)*0.25)
    start=jnp.sum(jnp.where(lanef<tcol,jnp.broadcast_to(g,(NBP,128)),0.0),axis=1,keepdims=True)
    pos=jnp.where(live,4.0*start+rank,-1.0).astype(jnp.int32)
    ident=iota((NBP,1),0).astype(f32)*64.0+bs_col+1.0
    hit=pos==iota((NBP,NSLOT),1)
    slots=jnp.sum(jnp.where(hit,jnp.broadcast_to(ident,(NBP,NSLOT)),0.0),axis=0,keepdims=True)
    l2=iota((128,128),1); s2=iota((128,128),0)
    gend=jnp.sum(jnp.where(l2<=s2,jnp.broadcast_to(g,(128,128)),0.0),axis=1,keepdims=True)
    gt=jnp.sum(jnp.where((s2<32)&(gend<=l2.astype(f32)),1.0,0.0),axis=0,keepdims=True)
    total=jnp.sum(g,axis=1,keepdims=True)
    return slots, jnp.where(iota((1,128),1)==127,jnp.broadcast_to(total,(1,128)),gt)

def begin_kernel(cnt, packed, obs_in, weight_in, prior_in, plan, w0, wgt, pri, obs, weight, prior, sem):
    small=[pltpu.make_async_copy(a,b,sem.at[k]) for k,(a,b) in enumerate(((prior_in,prior),(weight_in,weight),(obs_in,obs)))]
    for c in small: c.start()
    p=packed[...].astype(f32)
    q=p.T
    slots,gt=sort_blocks(cnt[0],p[0:1],q[:,0:1],q[:,1:2])
    plan[0:1]=slots.astype(jnp.int32)
    plan[1:2,0:128]=gt.astype(jnp.int32)
    for c in small: c.wait()
    pri[...]=jnp.broadcast_to(prior[...],(128,256)).T
    own=pl.multiple_of(8*lax.axis_index("region"),8)
    def spread(x): return jnp.broadcast_to(x,(128,64)).T
    mine=weight[pl.ds(own,8)]
    for k in range(8):
        wgt[k]=spread(mine[k:k+1])
    every=weight[...]
    for k in range(32):
        w0[k]=(spread(every[k:k+1])*obs[k]).astype(bf16)

SM=pl.BlockSpec(memory_space=pltpu.SMEM); VM=pl.BlockSpec(memory_space=pltpu.VMEM); HB=pl.BlockSpec(memory_space=pltpu.MemorySpace.HBM)
def begin(cnt, bs, bt, obs, weight, prior):
    packed=jnp.pad(jnp.stack([bt,bs]),((0,6),(0,NBP-NB)))
    return pl.pallas_call(begin_kernel,
        out_shape=(SH((2,NSLOT),jnp.int32),SH((32,64,128),bf16),SH((8,64,128)),SH((256,128))),
        in_specs=[SM,VM,HB,HB,HB],out_specs=(VM,)*4,
        scratch_shapes=[pltpu.VMEM((32,64,128),f32),pltpu.VMEM((32,64),f32),pltpu.VMEM((1,256),f32),pltpu.SemaphoreType.DMA((3,))],
        cost_estimate=pl.CostEstimate(flops=10**10,bytes_accessed=3*10**7,transcendentals=0),
        compiler_params=pltpu.CompilerParams(vmem_limit_bytes=10<<20),name="begin")(cnt,packed,obs,weight,prior)

def snd(plan,g,k):
    v=plan[0,4*g+k]
    return jnp.where(v==0,32,jnp.bitwise_and(v-1,63))
def group_loop(plan, body):
    turns=(plan[1,127]+(UN-1))//UN
    def turn(i,c):
        body(i)
        return c
    lax.fori_loop(0,turns,turn,0)
def four(plan,F,g):
    out=[]
    for k in range(4):
        v=plan[0,4*g+k]
        out.append(F[lax.shift_right_logical(jnp.maximum(v-1,0),6)])
    return jnp.concatenate(out,axis=0)

def t_kernel(plan, F, w, pa, pb, acc, wt0, wt1):
    lane=lax.broadcasted_iota(jnp.int32,(128,128),1)
    for p in range(16):
        x=jnp.concatenate([w[2*p],w[2*p+1]],axis=0).astype(f32).T
        y=pltpu.roll(x,64,1)
        lo=lane<64
        z=jnp.zeros_like(x)
        wt0[2*p]=jnp.where(lo,x,z).astype(bf16)
        wt1[2*p]=jnp.where(lo,z,y).astype(bf16)
        wt0[2*p+1]=jnp.where(lo,y,z).astype(bf16)
        wt1[2*p+1]=jnp.where(lo,z,x).astype(bf16)
    wt0[32]=jnp.zeros((128,128),bf16)
    wt1[32]=jnp.zeros((128,128),bf16)
    acc[...]=jnp.zeros_like(acc)
    def body(i):
        for j in range(UN):
            g=i*UN+j
            s=[snd(plan,g,k) for k in range(4)]
            lhs=jnp.concatenate([wt0[s[0]]+wt1[s[1]],wt0[s[2]]+wt1[s[3]]],axis=1)
            acc[plan[1,g]]+=jnp.dot(lhs,four(plan,F,g),preferred_element_type=f32)
    group_loop(plan,body)
    for y in range(4):
        for z in range(4):
            for c in range(2):
                x=acc[(y*4+z)*2+c].astype(pa.dtype)
                pa[c,z,y]=x[0:64]
                pb[c,y,z]=x[64:128]
def transpose_map(plan, F, w, dtype):
    o=SH((2,4,4,64,256),dtype)
    return pl.pallas_call(t_kernel,out_shape=(o,o),in_specs=[SM,VM,VM],out_specs=(VM,VM),
        scratch_shapes=[pltpu.VMEM((33,128,256),f32),pltpu.VMEM((33,128,128),bf16),pltpu.VMEM((33,128,128),bf16)],
        compiler_params=pltpu.CompilerParams(vmem_limit_bytes=24<<20), name="tmap")(plan,F,w)

def f_kernel(plan, F, va, vb, img, acc):
    acc[...]=jnp.zeros_like(acc)
    def body(i):
        for j in range(UN):
            g=i*UN+j
            t=jnp.minimum(plan[1,g],31)
            c=jnp.bitwise_and(t,1); z=jnp.bitwise_and(lax.shift_right_logical(t,1),3); y=lax.shift_right_logical(t,3)
            rhs=jnp.concatenate([va[c,z*4+y],vb[c,y*4+z]],axis=0)
            out=jnp.dot(four(plan,F,g),rhs,preferred_element_type=f32)
            for k in range(4):
                acc[snd(plan,g,k)]+=out[64*k:64*k+64]
    group_loop(plan,body)
    img[...]=acc[0:32].astype(img.dtype)
def forward_map(plan, F, va, vb):
    return pl.pallas_call(f_kernel,out_shape=SH((32,64,128),bf16),in_specs=[SM,VM,VM,VM],out_specs=VM,
        scratch_shapes=[pltpu.VMEM((33,64,128),f32)],
        compiler_params=pltpu.CompilerParams(vmem_limit_bytes=18<<20), name="fmap")(plan,F,va.reshape(2,16,128,128),vb.reshape(2,16,128,128))

MESH=pl.DeviceIdType.MESH
class Net:
    def __init__(self, send, recv):
        self.send, self.recv, self.ns, self.nr, self.owed = send, recv, 0, 0, []
    def sender(self, whole):
        k=self.ns; self.ns+=1
        self.owed.append((k,whole))
        return k
    def taker(self):
        k=self.nr; self.nr+=1
        return k
    def put(self, src, dst, dev, sk, rk):
        pltpu.make_async_remote_copy(src_ref=src,dst_ref=dst,send_sem=self.send.at[sk],recv_sem=self.recv.at[rk],device_id=dev,device_id_type=MESH).start()
    def take(self, rk, whole):
        pltpu.make_async_copy(whole,whole,self.recv.at[rk]).wait()
    def drain(self):
        for k,whole in self.owed:
            pltpu.make_async_copy(whole,whole,self.send.at[k]).wait()

def place():
    o=lax.axis_index("orbit"); r=lax.axis_index("region")
    return o//8,(o//2)%4,o%2,r
def dev(y,z,c,r): return (y*8+z*2+c, r)
def greet(devs):
    bar=pltpu.get_barrier_semaphore()
    for d in devs:
        pl.semaphore_signal(bar,inc=1,device_id=d,device_id_type=MESH)
    pl.semaphore_wait(bar,len(devs))

class Ring:
    def __init__(self, i, at):
        self.i=i
        self.to=[(i+d)%4 for d in range(4)]
        self.dev=[at((i+d)%4) for d in range(4)]
    def peers(self): return self.dev[1:4]
FAR=(2,1,3)

def reduce_scratch(dt, cdt):
    V=pltpu.VMEM
    return [V((4,4,64,256),cdt)]*2+[V((4,4,64,256),dt)]*2+[V((3,4,64,256),dt)]*2+[V((3,64,256),dt)]*4

def reduce_tiles(net, mate, c, ry, rz, pa, pb, sc, tick=lambda k:None):
    ra,rb,qa,qb,ga,gb,sa,sb,ha,hb=sc
    sides=((ry,rz,pa,ra,qa,ga,sa,ha),(rz,ry,pb,rb,qb,gb,sb,hb))
    order=(2,1,3,0)
    s0=[net.sender(r) for (m,n,p,r,q,g,s,h) in sides]
    k0=[[net.taker() for x in sides] for e in order]
    for k,e in enumerate(order):
        for b,(m,n,p,r,q,g,s,h) in enumerate(sides):
            net.put(p.at[1-c,n.to[e]],r.at[n.to[e]],mate,s0[b],k0[k][b])
    tick(0)
    s1=[net.sender(g) for (m,n,p,r,q,g,s,h) in sides]
    k1=[[net.taker() for x in sides] for e in order]
    for k,e in enumerate(order):
        for b,(m,n,p,r,q,g,s,h) in enumerate(sides):
            j=n.to[e]
            net.take(k0[k][b],r.at[j])
            for d in FAR:
                q[j,m.to[d]]=(p[c,j,m.to[d]].astype(f32)+r[j,m.to[d]].astype(f32)).astype(q.dtype)
                net.put(q.at[j,m.to[d]],g.at[d-1,j],m.dev[d],s1[b],k1[k][b])
    tick(1)
    s2=[net.sender(s) for (m,n,p,r,q,g,s,h) in sides]
    k2=[net.taker() for x in sides]
    own=[None,None]
    for k,e in enumerate(order):
        for b,(m,n,p,r,q,g,s,h) in enumerate(sides):
            j=n.to[e]
            x=p[c,j,m.i].astype(f32)+r[j,m.i].astype(f32)
            net.take(k1[k][b],h)
            x=x+(g[0,j].astype(f32)+g[1,j].astype(f32)+g[2,j].astype(f32))
            if e:
                s[e-1]=x.astype(s.dtype)
                net.put(s.at[e-1],h.at[e-1],n.dev[e],s2[b],k2[b])
            else: own[b]=x
    tick(2)
    for b,(m,n,p,r,q,g,s,h) in enumerate(sides):
        net.take(k2[b],h)
        own[b]=own[b]+(h[0].astype(f32)+h[1].astype(f32)+h[2].astype(f32))
    return jnp.concatenate(own,axis=0)

def gather_tiles(net, mate, c, ry, rz, va, vb, tick=lambda k:None):
    sides=((ry,rz,va),(rz,ry,vb))
    three=[v.at[0,0,pl.ds(0,3)] for m,n,v in sides]
    s1=[net.sender(x) for x in three]
    k1=[[net.taker() for d in range(3)] for x in sides]
    for b,(m,n,v) in enumerate(sides):
        s=v.at[c,n.i,m.i]
        for d in (1,3,2): net.put(s,s,n.dev[d],s1[b],k1[b][d-1])
    tick(0)
    s2=[net.sender(v.at[0,pl.ds(0,3)]) for m,n,v in sides]
    order=(0,3,1,2)
    k2=[[net.taker() for x in sides] for e in order]
    for k,e in enumerate(order):
        for b,(m,n,v) in enumerate(sides):
            s=v.at[c,n.to[e],m.i]
            if e: net.take(k1[b][3-e],s)
            for d in FAR: net.put(s,s,m.dev[d],s2[b],k2[k][b])
    tick(1)
    s3=[net.sender(v.at[0]) for m,n,v in sides]
    k3=[net.taker() for x in sides]
    for k,e in enumerate(order):
        for b,(m,n,v) in enumerate(sides):
            net.take(k2[k][b],three[b])
            s=v.at[c,n.to[e]]
            net.put(s,s,mate,s3[b],k3[b])
        if k==1: tick(2)
    tick(3)
    for b,(m,n,v) in enumerate(sides): net.take(k3[b],v.at[0])

class Reduce:
    def __init__(self, net, sin, sout, axes, base=0):
        self.net, self.sin, self.sout, self.axes = net, sin, sout, axes
        self.at=base; self.so=base; self.k=0
    def start(self, value):
        self.value=value
        self._send()
    def _send(self):
        a=self.axes[self.k]
        self.sout[self.so]=self.value
        sk=self.net.sender(self.sin.at[pl.ds(self.at,len(a))]); self.rk=self.net.taker()
        for i,d in enumerate(a): self.net.put(self.sout.at[self.so],self.sin.at[self.at+i],d,sk,self.rk)
    def step(self):
        n=len(self.axes[self.k])
        self.net.take(self.rk,self.sin.at[pl.ds(self.at,n)])
        for i in range(n): self.value=self.value+self.sin[self.at+i]
        self.at+=n; self.so+=1; self.k+=1
        if self.k<len(self.axes): self._send()
    def finish(self):
        while self.k<len(self.axes): self.step()
        return self.value
def rep(v): return jnp.broadcast_to(v,(8,128))

def first_kernel(pa, pb, prior, r0, va, vb, npl, *s):
    sc=s[:-4]; sin,sout,ssem,rsem=s[-4:]
    y,z,c,r=place(); mate=dev(y,z,1-c,r)
    ry=Ring(y,lambda i:dev(i,z,c,r)); rz=Ring(z,lambda i:dev(y,i,c,r))
    greet([mate]+ry.peers()+rz.peers())
    net=Net(ssem,rsem)
    t=reduce_tiles(net,mate,c,ry,rz,pa,pb,sc)
    res=prior[...]*t.T
    v=(prior[...]*res).astype(bf16)
    va[c,z,y]=v[0:128]; vb[c,y,z]=v[128:256]
    red=Reduce(net,sin,sout,[ry.peers(),rz.peers(),[mate]])
    def tick(k):
        if k==0:
            r0[...]=res
            red.start(rep(jnp.sum(res*res,axis=0,keepdims=True)))
        elif k>1: red.step()
    gather_tiles(net,mate,c,ry,rz,va,vb,tick)
    npl[...]=red.finish()
    net.drain()
    assert (net.ns,net.nr)==FIRST_NET, (net.ns,net.nr)

def mid_kernel(pa, pb, prior, r0, nrm, wi, r1, d1, it, nn, va, vb, dd, *s):
    sc=s[:-4]; sin,sout,ssem,rsem=s[-4:]
    y,z,c,r=place(); mate=dev(y,z,1-c,r)
    ry=Ring(y,lambda i:dev(i,z,c,r)); rz=Ring(z,lambda i:dev(y,i,c,r)); rx=Ring(r,lambda i:dev(y,z,c,i))
    greet([mate]+ry.peers()+rz.peers()+rx.peers())
    net=Net(ssem,rsem)
    plane=[ry.peers(),rz.peers(),[mate]]
    ra=Reduce(net,sin,sout,plane,0)
    def tick(k):
        if k==0: ra.start(wi[...])
        else: ra.step()
    t=reduce_tiles(net,mate,c,ry,rz,pa,pb,sc,tick)
    n0=nrm[0:1]
    step=n0/(n0+ra.finish()[0:1])
    d0=r0[...]
    res=d0-step*(d0+prior[...]*t.T)
    rb=Reduce(net,sin,sout,[[mate],rx.peers(),ry.peers(),rz.peers()],7)
    rb.start(rep(jnp.sum(res*res,axis=0,keepdims=True)))
    it[...]=step*d0
    r1[...]=res
    n1=rb.finish()
    nn[...]=n1
    d=res+(n1[0:1]/n0)*d0
    v=(prior[...]*d).astype(bf16)
    va[c,z,y]=v[0:128]; vb[c,y,z]=v[128:256]
    rc=Reduce(net,sin,sout,plane,17)
    def tick2(k):
        if k==0:
            d1[...]=d
            rc.start(rep(jnp.sum(d*d,axis=0,keepdims=True)))
        elif k>1: rc.step()
    gather_tiles(net,mate,c,ry,rz,va,vb,tick2)
    dd[...]=rc.finish()
    net.drain()
    assert (net.ns,net.nr)==MID_NET, (net.ns,net.nr)

def last_kernel(pa, pb, prior, r1, d1, it, n1, dd, wi, flux, resid, *s):
    sc=s[:-4]; sin,sout,ssem,rsem=s[-4:]
    y,z,c,r=place(); mate=dev(y,z,1-c,r)
    ry=Ring(y,lambda i:dev(i,z,c,r)); rz=Ring(z,lambda i:dev(y,i,c,r))
    greet([mate]+ry.peers()+rz.peers())
    net=Net(ssem,rsem)
    ra=Reduce(net,sin,sout,[ry.peers(),rz.peers(),[mate]],0)
    def tick(k):
        if k==0: ra.start(wi[...])
        else: ra.step()
    t=reduce_tiles(net,mate,c,ry,rz,pa,pb,sc,tick)
    step=n1[0:1]/(dd[0:1]+ra.finish()[0:1])
    p=d1[...]+prior[...]*t.T
    resid[...]=r1[...]-step*p
    flux[...]=prior[...]*(it[...]+step*d1[...])
    net.drain()
    assert (net.ns,net.nr)==LAST_NET, (net.ns,net.nr)

CH=4
def cross_kernel(img, wgt, part, w, tot, wi, g, ri, so, sin, sout, ssem, rsem):
    y,z,c,r=place()
    rx=Ring(r,lambda i:dev(y,z,c,i))
    greet(rx.peers())
    net=Net(ssem,rsem)
    n=8//CH
    B=[pl.ds(j*n,n) for j in range(CH)]
    way=lambda j: 1 if j%2==0 else 3
    sf,sn,sv=net.sender(ri),net.sender(ri),net.sender(ri)
    kf=[net.taker() for j in range(CH)]; kn=[net.taker() for j in range(CH)]
    for j in range(CH): net.put(img.at[rx.to[2],B[j]],ri.at[j],rx.dev[way(j)],sf,kf[j])
    for j in range(CH): net.put(img.at[rx.to[4-way(j)],B[j]],g.at[1 if way(j)==1 else 0,B[j]],rx.dev[4-way(j)],sn,kn[j])
    ra=Reduce(net,sin,sout,[rx.peers()],0)
    ra.start(part[...])
    for j in range(CH):
        net.take(kf[j],ri.at[j])
        so[j]=(img[rx.to[way(j)],B[j]].astype(f32)+ri[j].astype(f32)).astype(bf16)
        net.put(so.at[j],g.at[0 if way(j)==1 else 1,B[j]],rx.dev[way(j)],sv,kn[j])
    sums=jnp.zeros((64,128),f32)
    sa,sr=net.sender(w.at[pl.ds(0,2)]),net.sender(w.at[0])
    ka=[net.taker() for j in range(CH)]; kr=net.taker()
    for j in range(CH):
        b=B[j]
        net.take(kn[j],g.at[0,pl.ds(0,2*n)])
        x=img[r,b].astype(f32)+(g[0,b].astype(f32)+g[1,b].astype(f32))
        m=wgt[b]*x
        w[r,b]=m.astype(bf16)
        s=w.at[r,b]
        net.put(s,s,rx.dev[way(j)],sa,ka[j])
        net.put(s,s,rx.dev[4-way(j)],sa,kr)
        sums=sums+jnp.sum(m*x,axis=0)
    rb=Reduce(net,sin,sout,[rx.peers()],3)
    rb.start(rep(jnp.sum(sums,axis=0,keepdims=True)))
    for j in range(CH):
        s=w.at[rx.to[4-way(j)],B[j]]
        net.take(ka[j],s)
        net.put(s,s,rx.dev[way(j)],sr,kr)
    tot[...]=ra.finish()
    wi[...]=rb.finish()
    net.take(kr,w.at[pl.ds(0,2)])
    net.drain()
    assert (net.ns,net.nr)==CROSS_NET, (net.ns,net.nr)

FIRST_NET=(15,37); MID_NET=(22,44); LAST_NET=(9,21); CROSS_NET=(7,15)
def _call(kernel, outs, scratch, cid, lim, name, *args):
    return pl.pallas_call(kernel,out_shape=outs,in_specs=[VM]*len(args),out_specs=tuple([VM]*len(outs)),
        scratch_shapes=scratch,compiler_params=pltpu.CompilerParams(collective_id=cid,has_side_effects=True,vmem_limit_bytes=lim<<20),name=name)(*args)
VA=SH((2,4,4,128,128),bf16); ROW=SH((8,128)); TILE=SH((256,128))
def tail(n, net): return [pltpu.VMEM((n,8,128),f32)]*2+[pltpu.SemaphoreType.DMA((k,)) for k in net]
def first(pa,pb,prior):
    return _call(first_kernel,[TILE,VA,VA,ROW],reduce_scratch(f32,f32)+tail(7,FIRST_NET),0,22,"first",pa,pb,prior)
def mid(pa,pb,prior,r0,nrm,wi):
    return _call(mid_kernel,[TILE,TILE,TILE,ROW,VA,VA,ROW],reduce_scratch(bf16,pa.dtype)+tail(24,MID_NET),1,18,"mid",pa,pb,prior,r0,nrm,wi)
def last(pa,pb,prior,r1,d1,it,n1,dd,wi):
    return _call(last_kernel,[TILE,TILE],reduce_scratch(bf16,pa.dtype)+tail(7,LAST_NET),2,14,"last",pa,pb,prior,r1,d1,it,n1,dd,wi)
def cross(img,wgt,part):
    return _call(cross_kernel,[SH((4,8,64,128),bf16),ROW,ROW],[pltpu.VMEM((2,8,64,128),bf16),pltpu.VMEM((CH,8//CH,64,128),bf16),pltpu.VMEM((CH,8//CH,64,128),bf16)]+tail(6,CROSS_NET),3,8,"cross",img.reshape(4,8,64,128),wgt,part)

def per_device(footprints, block_sounding, block_tile, block_count, observations, obs_weight, prior_std):
    F = footprints
    plan, w0, wgt, prior = begin(block_count, block_sounding, block_tile, observations, obs_weight, prior_std.reshape(1, 256))
    pa, pb = transpose_map(plan, F, w0, f32)
    r0, va, vb, norm = first(pa, pb, prior)
    img = forward_map(plan, F, va, vb)
    w, norm, wi = cross(img, wgt, norm)
    pa, pb = transpose_map(plan, F, w.reshape(32, 64, 128), f32)
    r1, d1, it, n1, va, vb, dd = mid(pa, pb, prior, r0, norm, wi)
    img = forward_map(plan, F, va, vb)
    w, dd, wi = cross(img, wgt, dd)
    pa, pb = transpose_map(plan, F, w.reshape(32, 64, 128), bf16)
    flux, resid = last(pa, pb, prior, r1, d1, it, n1, dd, wi)
    return flux[None, None], resid[None, None]


def solution(mesh):
    return jax.shard_map(
        per_device,
        mesh=mesh,
        in_specs=(
            P(("orbit", "region"), None, None),
            P(("orbit", "region")),
            P(("orbit", "region")),
            P(("orbit", "region")),
            P("orbit", None, None),
            P("orbit", None),
            P("region", "orbit", None),
        ),
        out_specs=(P("region", "orbit", None, None), P("region", "orbit", None, None)),
        check_vma=False,
    )
```

time: 1180 us -> 158 us (0.13)
  waiting for transfers between devices: 530 us -> 0 us
  other arithmetic: 284 us -> 0.01 us
  blocking collectives: 195 us -> 0 us
  Pallas kernels: 0 us -> 149 us
  matrix products: 103 us -> 0 us
  local copies, waits for them, and re-layouts: 55.5 us -> 7.06 us
  between operations: 14.9 us -> 1.4 us
    reduce_scatter x3 -> x0, waiting for transfers between devices: 331 us -> none  [reduce_tiles(): lax.psum_scatter(partial_value, 'orbit', scatter_dimension=0, tiled=True)]
    scatter-add x20 -> x0, other arithmetic: 257 us -> none  [the longest x12 227 us: turn(): jax.ops.segment_sum(contrib, targets, num_segments=tile_count)]
    psum x3 -> x0, blocking collectives: 195 us -> none  [inner_sum(): lax.psum(jnp.sum(first_vec * second_vec, axis=(0, 1)), ('orbit', 'region'))]
    pallas_call x0 -> x11, Pallas kernels: none -> 149 us  [the longest x5 128 us: _call(): pl.pallas_call(kernel, out_shape=outs, in_specs=[VM] * len(args), out_spe...]
    psum x2 -> x0, waiting for transfers between devices: 112 us -> none  [per_device(): image = lax.psum(partial_value, 'region')]
    dot_general x20 -> x0, matrix products: 103 us -> none  [the longest x12 73.4 us: turn(): jnp.einsum('bsc,bsr->bcr', blocks_now, weighted[sound_ids], preferred_ele...]
    all_gather x2 -> x0, waiting for transfers between devices: 87.6 us -> none  [per_device(): lax.all_gather(scaled, 'orbit', axis=0, tiled=True)]
    gather x20 -> x0, local copies, waits for them, and re-layouts: 45.8 us -> none  [the longest x8 36.8 us: turn(): whole[tile_ids]]
  transfers between devices with their start and end apart: 7 -> 0, of which waited for: 7 -> 0; matrix products, arithmetic and copies ran while one was open for 0% -> 0% of each run, Pallas kernels for 0% -> 0%
where the time goes in v2:
time: 158 us
  Pallas kernels  149 us (94%)
  local copies, waits for them, and re-layouts  7.06 us (4%)
    pallas_call x5, Pallas kernels, _call(): pl.pallas_call(kernel, out_shape=outs, in_specs=[VM] * len(args), out_spe...  128 us
    pallas_call x3, Pallas kernels, transpose_map(): pl.pallas_call(t_kernel, out_shape=(o, o), in_specs=[SM, VM, VM], out_spe...  12.4 us
    pallas_call x2, Pallas kernels, forward_map(): pl.pallas_call(f_kernel, out_shape=SH((32, 64, 128), bf16), in_specs=[SM,...  7.47 us
    unnamed x14, local copies, waits for them, and re-layouts  5.68 us

profile of v2, /device:TPU:1, one launch (start us, length us, event | category | flops | bytes accessed | tf_op | source)
XLA Modules:
  0.0 157.9 jit_solution(14855917937027855584)
XLA Ops:
  1.3 0.7 stack.10
  2.0 0.7 stack.9
  2.7 0.0 slice-start
  2.7 0.0 copy-start
  2.7 1.4 copy-done
  4.1 0.0 copy-start.1
  4.1 0.9 copy-done.1
  5.0 0.0 copy-start.2
  5.0 0.7 copy-done.2
  5.6 0.0 slice-start.1
  5.6 0.0 slice-start.2
  5.6 1.4 begin.1
  7.1 0.0 slice-done
  7.1 0.7 slice-done.1
  7.8 0.7 slice-done.2
  8.5 4.2 %tmap.3 = (f32[2,4,4,64,256]{4,3,2,1,0:T(8,128)S(1)}, f32[2,4,4,64,256]{4,3,2,1,0:T(8,128)S(1)}) custom-call(s32[2,512]{1,0:T(2,128)S(1)} %get-tuple-element.31.plan, bf16[320,64,256]{2,1,0:T(8,128)(2,1)S(1)} %bitcast.12, bf16[32,64,128]{2,1,0:T(8,128)(2,1)S(1)} %get-tuple-element.32.w), custom_call_target="tpu_custom_call" | custom-call | tf_op jit(solution)/shard_map/tmap/pallas_call | solution.py:109
  12.7 39.2 %first.1 = (f32[256,128]{1,0:T(8,128)S(1)}, bf16[2,4,4,128,128]{4,3,2,1,0:T(8,128)(2,1)S(1)}, bf16[2,4,4,128,128]{4,3,2,1,0:T(8,128)(2,1)S(1)}, f32[8,128]{1,0:T(8,128)S(1)}) custom-call(f32[2,4,4,64,256]{4,3,2,1,0:T(8,128)S(1)} %get-tuple-element.33.pa, f32[2,4,4,64,256]{4,3,2,1,0:T(8,128)S(1)} %get-tuple-element.34.pb, f32[256,128]{1,0:T(8,128)S(1)} %get-tuple-element.35.prior), custom_call_target="tpu_custom_call" | custom-call | tf_op jit(solution)/shard_map/first/pallas_call | solution.py:384
  51.8 3.7 %fmap.2 = bf16[32,64,128]{2,1,0:T(8,128)(2,1)S(1)} custom-call(s32[2,512]{1,0:T(2,128)S(1)} %get-tuple-element.31.plan, bf16[320,64,256]{2,1,0:T(8,128)(2,1)S(1)} %bitcast.12, bf16[2,16,128,128]{3,2,1,0:T(8,128)(2,1)S(1)} %bitcast.17, bf16[2,16,128,128]{3,2,1,0:T(8,128)(2,1)S(1)} %bitcast.18), custom_call_target="tpu_custom_call" | custom-call | tf_op jit(solution)/shard_map/fmap/pallas_call | solution.py:127
  55.6 16.0 %cross.2 = (bf16[4,8,64,128]{3,2,1,0:T(8,128)(2,1)S(1)}, f32[8,128]{1,0:T(8,128)S(1)}, f32[8,128]{1,0:T(8,128)S(1)}) custom-call(bf16[4,8,64,128]{3,2,1,0:T(8,128)(2,1)S(1)} %bitcast.14, f32[8,64,128]{2,1,0:T(8,128)S(1)} %get-tuple-element.38.wgt, f32[8,128]{1,0:T(8,128)S(1)} %get-tuple-element.39.part), custom_call_target="tpu_custom_call" | custom-call | tf_op jit(solution)/shard_map/cross/pallas_call | solution.py:384
  71.6 4.2 %tmap.4 = (f32[2,4,4,64,256]{4,3,2,1,0:T(8,128)S(1)}, f32[2,4,4,64,256]{4,3,2,1,0:T(8,128)S(1)}) custom-call(s32[2,512]{1,0:T(2,128)S(1)} %get-tuple-element.31.plan, bf16[320,64,256]{2,1,0:T(8,128)(2,1)S(1)} %bitcast.12, bf16[32,64,128]{2,1,0:T(8,128)(2,1)S(1)} %bitcast.20), custom_call_target="tpu_custom_call" | custom-call | tf_op jit(solution)/shard_map/tmap/pallas_call | solution.py:109
  75.8 41.8 %mid.1 = (f32[256,128]{1,0:T(8,128)S(1)}, f32[256,128]{1,0:T(8,128)S(1)}, f32[256,128]{1,0:T(8,128)S(1)}, f32[8,128]{1,0:T(8,128)S(1)}, bf16[2,4,4,128,128]{4,3,...) custom-call(f32[2,4,4,64,256]{4,3,2,1,0:T(8,128)S(1)} %get-tuple-element.41.pa, ...), custom_call_target="tpu_custom_call" | custom-call | tf_op jit(solution)/shard_map/mid/pallas_call | solution.py:384
  117.6 3.8 %fmap.3 = bf16[32,64,128]{2,1,0:T(8,128)(2,1)S(1)} custom-call(s32[2,512]{1,0:T(2,128)S(1)} %get-tuple-element.31.plan, bf16[320,64,256]{2,1,0:T(8,128)(2,1)S(1)} %bitcast.12, bf16[2,16,128,128]{3,2,1,0:T(8,128)(2,1)S(1)} %bitcast.15, bf16[2,16,128,128]{3,2,1,0:T(8,128)(2,1)S(1)} %bitcast.16), custom_call_target="tpu_custom_call" | custom-call | tf_op jit(solution)/shard_map/fmap/pallas_call | solution.py:127
  121.3 15.0 %cross.3 = (bf16[4,8,64,128]{3,2,1,0:T(8,128)(2,1)S(1)}, f32[8,128]{1,0:T(8,128)S(1)}, f32[8,128]{1,0:T(8,128)S(1)}) custom-call(bf16[4,8,64,128]{3,2,1,0:T(8,128)(2,1)S(1)} %bitcast.13, f32[8,64,128]{2,1,0:T(8,128)S(1)} %get-tuple-element.38.wgt, f32[8,128]{1,0:T(8,128)S(1)} %get-tuple-element.48.part), custom_call_target="tpu_custom_call" | custom-call | tf_op jit(solution)/shard_map/cross/pallas_call | solution.py:384
  136.4 4.1 %tmap.5 = (bf16[2,4,4,64,256]{4,3,2,1,0:T(8,128)(2,1)S(1)}, bf16[2,4,4,64,256]{4,3,2,1,0:T(8,128)(2,1)S(1)}) custom-call(s32[2,512]{1,0:T(2,128)S(1)} %get-tuple-element.31.plan, bf16[320,64,256]{2,1,0:T(8,128)(2,1)S(1)} %bitcast.12, bf16[32,64,128]{2,1,0:T(8,128)(2,1)S(1)} %bitcast.19), custom_call_target="tpu_custom_call" | custom-call | tf_op jit(solution)/shard_map/tmap/pallas_call | solution.py:109
  140.5 16.1 %last.1 = (f32[256,128]{1,0:T(8,128)S(1)}, f32[256,128]{1,0:T(8,128)S(1)}) custom-call(bf16[2,4,4,64,256]{4,3,2,1,0:T(8,128)(2,1)S(1)} %get-tuple-element.50.pa, bf16[2,4,4,64,256]{4,3,2,1,0:T(8,128)(2,1)S(1)} %get-tuple-element.51.pb, f32[256,128]{1,0:T(8,128)S(1)} %get-tuple-element.35.prior, f32[256,128]{1,0:T(8,128)S(1)} %get-tuple-element.52.r1, ...), custom_call_target="tpu_custom_call" | custom-call | tf_op jit(solution)/shard_map/last/pallas_call | solution.py:384
  156.6 0.7 copy.12
  157.3 0.7 copy.13
  (3 shorter events, 0.0 us)
Async XLA Ops:
  2.7 4.4 %slice-start = ((s8[10485760]{0:T(1024)(128)(4,1)}), s8[4194304]{0:T(1024)(128)(4,1)S(1)}, s32[]{:S(2)}) async-start(s8[10485760]{0:T(1024)(128)(4,1)} %bitcast.11), calls=%async_computation | async-start | bytes 8388608
  2.7 1.4 copy-start
  4.1 0.9 copy-start.1
  5.0 0.7 copy-start.2
  5.6 2.2 %slice-start.1 = ((s8[10485760]{0:T(1024)(128)(4,1)}), s8[4194304]{0:T(1024)(128)(4,1)S(1)}, s32[]{:S(2)}) async-start(s8[10485760]{0:T(1024)(128)(4,1)} %bitcast.11), calls=%async_computation.1 | async-start | bytes 8388608
  5.6 2.9 %slice-start.2 = ((s8[10485760]{0:T(1024)(128)(4,1)}), s8[2097152]{0:T(1024)(128)(4,1)S(1)}, s32[]{:S(2)}) async-start(s8[10485760]{0:T(1024)(128)(4,1)} %bitcast.11), calls=%async_computation.2 | async-start | bytes 4194304

commit v3 on v2

--- a/solution.py
+++ b/solution.py
@@ -9,7 +9,7 @@
 bf16 = jnp.bfloat16
 def SH(shape, dtype=f32): return jax.ShapeDtypeStruct(shape, dtype)
 
-NB=320; NBP=384; NSLOT=512; UN=16; NCH=4
+NB=320; NBP=384; NSLOT=512; UN=24; NCH=4
 
 def sort_blocks(n, bt_row, bt_col, bs_col):
     iota=lambda shape,d: lax.broadcasted_iota(jnp.int32, shape, d)
@@ -32,15 +32,14 @@
     total=jnp.sum(g,axis=1,keepdims=True)
     return slots, jnp.where(iota((1,128),1)==127,jnp.broadcast_to(total,(1,128)),gt)
 
-def begin_kernel(cnt, packed, obs_in, weight_in, prior_in, plan, w0, wgt, pri, obs, weight, prior, sem):
-    small=[pltpu.make_async_copy(a,b,sem.at[k]) for k,(a,b) in enumerate(((prior_in,prior),(weight_in,weight),(obs_in,obs)))]
-    for c in small: c.start()
+def sort_kernel(cnt, packed, plan):
     p=packed[...].astype(f32)
     q=p.T
     slots,gt=sort_blocks(cnt[0],p[0:1],q[:,0:1],q[:,1:2])
     plan[0:1]=slots.astype(jnp.int32)
     plan[1:2,0:128]=gt.astype(jnp.int32)
-    for c in small: c.wait()
+
+def spread_kernel(obs, weight, prior, w0, wgt, pri):
     pri[...]=jnp.broadcast_to(prior[...],(128,256)).T
     own=pl.multiple_of(8*lax.axis_index("region"),8)
     def spread(x): return jnp.broadcast_to(x,(128,64)).T
@@ -51,15 +50,17 @@
     for k in range(32):
         w0[k]=(spread(every[k:k+1])*obs[k]).astype(bf16)
 
-SM=pl.BlockSpec(memory_space=pltpu.SMEM); VM=pl.BlockSpec(memory_space=pltpu.VMEM); HB=pl.BlockSpec(memory_space=pltpu.MemorySpace.HBM)
+SM=pl.BlockSpec(memory_space=pltpu.SMEM); VM=pl.BlockSpec(memory_space=pltpu.VMEM)
 def begin(cnt, bs, bt, obs, weight, prior):
     packed=jnp.pad(jnp.stack([bt,bs]),((0,6),(0,NBP-NB)))
-    return pl.pallas_call(begin_kernel,
-        out_shape=(SH((2,NSLOT),jnp.int32),SH((32,64,128),bf16),SH((8,64,128)),SH((256,128))),
-        in_specs=[SM,VM,HB,HB,HB],out_specs=(VM,)*4,
-        scratch_shapes=[pltpu.VMEM((32,64,128),f32),pltpu.VMEM((32,64),f32),pltpu.VMEM((1,256),f32),pltpu.SemaphoreType.DMA((3,))],
+    plan=pl.pallas_call(sort_kernel,out_shape=SH((2,NSLOT),jnp.int32),in_specs=[SM,VM],out_specs=VM,
         cost_estimate=pl.CostEstimate(flops=10**10,bytes_accessed=3*10**7,transcendentals=0),
-        compiler_params=pltpu.CompilerParams(vmem_limit_bytes=10<<20),name="begin")(cnt,packed,obs,weight,prior)
+        compiler_params=pltpu.CompilerParams(vmem_limit_bytes=8<<20),name="sort")(cnt,packed)
+    w0,wgt,pri=pl.pallas_call(spread_kernel,out_shape=(SH((32,64,128),bf16),SH((8,64,128)),SH((256,128))),
+        in_specs=[VM]*3,out_specs=(VM,)*3,
+        cost_estimate=pl.CostEstimate(flops=10**9,bytes_accessed=4*10**6,transcendentals=0),
+        compiler_params=pltpu.CompilerParams(vmem_limit_bytes=8<<20),name="spread")(obs,weight,prior)
+    return plan,w0,wgt,pri
 
 def snd(plan,g,k):
     v=plan[0,4*g+k]
@@ -163,7 +164,7 @@
         self.to=[(i+d)%4 for d in range(4)]
         self.dev=[at((i+d)%4) for d in range(4)]
     def peers(self): return self.dev[1:4]
-FAR=(2,1,3)
+FAR=(1,3,2)
 
 def reduce_scratch(dt, cdt):
     V=pltpu.VMEM
@@ -285,7 +286,8 @@
     sc=s[:-4]; sin,sout,ssem,rsem=s[-4:]
     y,z,c,r=place(); mate=dev(y,z,1-c,r)
     ry=Ring(y,lambda i:dev(i,z,c,r)); rz=Ring(z,lambda i:dev(y,i,c,r)); rx=Ring(r,lambda i:dev(y,z,c,i))
-    greet([mate]+ry.peers()+rz.peers()+rx.peers())
+    here=rx.peers()+[mate]+[dev(y,z,1-c,x) for x in rx.to[1:]]
+    greet(here+ry.peers()+rz.peers())
     net=Net(ssem,rsem)
     plane=[ry.peers(),rz.peers(),[mate]]
     ra=Reduce(net,sin,sout,plane,0)
@@ -297,7 +299,7 @@
     step=n0/(n0+ra.finish()[0:1])
     d0=r0[...]
     res=d0-step*(d0+prior[...]*t.T)
-    rb=Reduce(net,sin,sout,[[mate],rx.peers(),ry.peers(),rz.peers()],7)
+    rb=Reduce(net,sin,sout,[here,ry.peers(),rz.peers()],7)
     rb.start(rep(jnp.sum(res*res,axis=0,keepdims=True)))
     it[...]=step*d0
     r1[...]=res
@@ -306,7 +308,7 @@
     d=res+(n1[0:1]/n0)*d0
     v=(prior[...]*d).astype(bf16)
     va[c,z,y]=v[0:128]; vb[c,y,z]=v[128:256]
-    rc=Reduce(net,sin,sout,plane,17)
+    rc=Reduce(net,sin,sout,plane,20)
     def tick2(k):
         if k==0:
             d1[...]=d
@@ -317,7 +319,7 @@
     net.drain()
     assert (net.ns,net.nr)==MID_NET, (net.ns,net.nr)
 
-def last_kernel(pa, pb, prior, r1, d1, it, n1, dd, wi, flux, resid, *s):
+def last_kernel(pa, pb, n1, dd, wi, back, step, *s):
     sc=s[:-4]; sin,sout,ssem,rsem=s[-4:]
     y,z,c,r=place(); mate=dev(y,z,1-c,r)
     ry=Ring(y,lambda i:dev(i,z,c,r)); rz=Ring(z,lambda i:dev(y,i,c,r))
@@ -328,58 +330,45 @@
         if k==0: ra.start(wi[...])
         else: ra.step()
     t=reduce_tiles(net,mate,c,ry,rz,pa,pb,sc,tick)
-    step=n1[0:1]/(dd[0:1]+ra.finish()[0:1])
-    p=d1[...]+prior[...]*t.T
-    resid[...]=r1[...]-step*p
-    flux[...]=prior[...]*(it[...]+step*d1[...])
+    step[...]=n1[...]/(dd[...]+ra.finish())
+    back[...]=t.T
     net.drain()
     assert (net.ns,net.nr)==LAST_NET, (net.ns,net.nr)
 
 CH=4
-def cross_kernel(img, wgt, part, w, tot, wi, g, ri, so, sin, sout, ssem, rsem):
+def cross_kernel(img, wgt, part, w, tot, wi, g, sin, sout, ssem, rsem):
     y,z,c,r=place()
     rx=Ring(r,lambda i:dev(y,z,c,i))
     greet(rx.peers())
     net=Net(ssem,rsem)
     n=8//CH
     B=[pl.ds(j*n,n) for j in range(CH)]
-    way=lambda j: 1 if j%2==0 else 3
-    sf,sn,sv=net.sender(ri),net.sender(ri),net.sender(ri)
-    kf=[net.taker() for j in range(CH)]; kn=[net.taker() for j in range(CH)]
-    for j in range(CH): net.put(img.at[rx.to[2],B[j]],ri.at[j],rx.dev[way(j)],sf,kf[j])
-    for j in range(CH): net.put(img.at[rx.to[4-way(j)],B[j]],g.at[1 if way(j)==1 else 0,B[j]],rx.dev[4-way(j)],sn,kn[j])
+    s1=net.sender(g); k1=[net.taker() for j in range(CH)]
+    for j in range(CH):
+        for d in FAR: net.put(img.at[rx.to[d],B[j]],g.at[d-1,B[j]],rx.dev[d],s1,k1[j])
     ra=Reduce(net,sin,sout,[rx.peers()],0)
     ra.start(part[...])
-    for j in range(CH):
-        net.take(kf[j],ri.at[j])
-        so[j]=(img[rx.to[way(j)],B[j]].astype(f32)+ri[j].astype(f32)).astype(bf16)
-        net.put(so.at[j],g.at[0 if way(j)==1 else 1,B[j]],rx.dev[way(j)],sv,kn[j])
     sums=jnp.zeros((64,128),f32)
-    sa,sr=net.sender(w.at[pl.ds(0,2)]),net.sender(w.at[0])
-    ka=[net.taker() for j in range(CH)]; kr=net.taker()
+    s2=net.sender(g); k2=net.taker()
     for j in range(CH):
         b=B[j]
-        net.take(kn[j],g.at[0,pl.ds(0,2*n)])
-        x=img[r,b].astype(f32)+(g[0,b].astype(f32)+g[1,b].astype(f32))
+        x=img[r,b].astype(f32)
+        net.take(k1[j],g.at[pl.ds(0,3),pl.ds(0,n)])
+        x=x+(g[0,b].astype(f32)+g[1,b].astype(f32)+g[2,b].astype(f32))
         m=wgt[b]*x
         w[r,b]=m.astype(bf16)
         s=w.at[r,b]
-        net.put(s,s,rx.dev[way(j)],sa,ka[j])
-        net.put(s,s,rx.dev[4-way(j)],sa,kr)
+        for d in FAR: net.put(s,s,rx.dev[d],s2,k2)
         sums=sums+jnp.sum(m*x,axis=0)
     rb=Reduce(net,sin,sout,[rx.peers()],3)
     rb.start(rep(jnp.sum(sums,axis=0,keepdims=True)))
-    for j in range(CH):
-        s=w.at[rx.to[4-way(j)],B[j]]
-        net.take(ka[j],s)
-        net.put(s,s,rx.dev[way(j)],sr,kr)
     tot[...]=ra.finish()
     wi[...]=rb.finish()
-    net.take(kr,w.at[pl.ds(0,2)])
+    net.take(k2,g)
     net.drain()
     assert (net.ns,net.nr)==CROSS_NET, (net.ns,net.nr)
 
-FIRST_NET=(15,37); MID_NET=(22,44); LAST_NET=(9,21); CROSS_NET=(7,15)
+FIRST_NET=(15,37); MID_NET=(21,43); LAST_NET=(9,21); CROSS_NET=(4,CH+3)
 def _call(kernel, outs, scratch, cid, lim, name, *args):
     return pl.pallas_call(kernel,out_shape=outs,in_specs=[VM]*len(args),out_specs=tuple([VM]*len(outs)),
         scratch_shapes=scratch,compiler_params=pltpu.CompilerParams(collective_id=cid,has_side_effects=True,vmem_limit_bytes=lim<<20),name=name)(*args)
@@ -388,11 +377,11 @@
 def first(pa,pb,prior):
     return _call(first_kernel,[TILE,VA,VA,ROW],reduce_scratch(f32,f32)+tail(7,FIRST_NET),0,22,"first",pa,pb,prior)
 def mid(pa,pb,prior,r0,nrm,wi):
-    return _call(mid_kernel,[TILE,TILE,TILE,ROW,VA,VA,ROW],reduce_scratch(bf16,pa.dtype)+tail(24,MID_NET),1,18,"mid",pa,pb,prior,r0,nrm,wi)
-def last(pa,pb,prior,r1,d1,it,n1,dd,wi):
-    return _call(last_kernel,[TILE,TILE],reduce_scratch(bf16,pa.dtype)+tail(7,LAST_NET),2,14,"last",pa,pb,prior,r1,d1,it,n1,dd,wi)
+    return _call(mid_kernel,[TILE,TILE,TILE,ROW,VA,VA,ROW],reduce_scratch(bf16,pa.dtype)+tail(27,MID_NET),1,18,"mid",pa,pb,prior,r0,nrm,wi)
+def last(pa,pb,n1,dd,wi):
+    return _call(last_kernel,[TILE,ROW],reduce_scratch(bf16,pa.dtype)+tail(7,LAST_NET),2,14,"last",pa,pb,n1,dd,wi)
 def cross(img,wgt,part):
-    return _call(cross_kernel,[SH((4,8,64,128),bf16),ROW,ROW],[pltpu.VMEM((2,8,64,128),bf16),pltpu.VMEM((CH,8//CH,64,128),bf16),pltpu.VMEM((CH,8//CH,64,128),bf16)]+tail(6,CROSS_NET),3,8,"cross",img.reshape(4,8,64,128),wgt,part)
+    return _call(cross_kernel,[SH((4,8,64,128),bf16),ROW,ROW],[pltpu.VMEM((3,8,64,128),bf16)]+tail(6,CROSS_NET),3,8,"cross",img.reshape(4,8,64,128),wgt,part)
 
 def per_device(footprints, block_sounding, block_tile, block_count, observations, obs_weight, prior_std):
     F = footprints
@@ -406,7 +395,10 @@
     img = forward_map(plan, F, va, vb)
     w, dd, wi = cross(img, wgt, dd)
     pa, pb = transpose_map(plan, F, w.reshape(32, 64, 128), bf16)
-    flux, resid = last(pa, pb, prior, r1, d1, it, n1, dd, wi)
+    back, step = last(pa, pb, n1, dd, wi)
+    step = step[0:1]
+    resid = r1 - step * (d1 + prior * back)
+    flux = prior * (it + step * d1)
     return flux[None, None], resid[None, None]
 
 

time: 158 us -> 156 us (0.987)
  local copies, waits for them, and re-layouts: 7.06 us -> 4.39 us
    unnamed x14 -> x12, local copies, waits for them, and re-layouts: 5.68 us -> 3.02 us
where the time goes in v3:
time: 156 us
  Pallas kernels  149 us (96%)
  local copies, waits for them, and re-layouts  4.39 us (3%)
    pallas_call x5, Pallas kernels, _call(): pl.pallas_call(kernel, out_shape=outs, in_specs=[VM] * len(args), out_spe...  127 us
    pallas_call x3, Pallas kernels, transpose_map(): pl.pallas_call(t_kernel, out_shape=(o, o), in_specs=[SM, VM, VM], out_spe...  13.1 us
    pallas_call x2, Pallas kernels, forward_map(): pl.pallas_call(f_kernel, out_shape=SH((32, 64, 128), bf16), in_specs=[SM,...  7.7 us

profile of v3, /device:TPU:1, one launch (start us, length us, event | category | flops | bytes accessed | tf_op | source)
XLA Modules:
  0.0 156.0 jit_solution(11499778077391226287)
XLA Ops:
  1.3 0.7 stack.10
  2.0 0.7 stack.9
  2.7 0.0 slice-start
  2.7 0.0 copy-start
  2.7 0.0 copy-start.1
  2.7 0.0 copy-start.2
  2.7 0.0 slice-start.1
  2.7 0.0 slice-start.2
  2.7 0.6 sort.1.plan
  3.3 0.8 copy-done
  4.1 0.0 copy-done.1
  4.1 0.0 copy-done.2
  4.1 0.8 spread.1
  4.8 0.4 slice-done
  5.2 1.3 slice-done.1
  6.5 0.6 slice-done.2
  7.1 4.4 %tmap.3 = (f32[2,4,4,64,256]{4,3,2,1,0:T(8,128)S(1)}, f32[2,4,4,64,256]{4,3,2,1,0:T(8,128)S(1)}) custom-call(s32[2,512]{1,0:T(2,128)S(1)} %sort.1.plan, bf16[320,64,256]{2,1,0:T(8,128)(2,1)S(1)} %bitcast.16, bf16[32,64,128]{2,1,0:T(8,128)(2,1)S(1)} %get-tuple-element.31.w), custom_call_target="tpu_custom_call" | custom-call | tf_op jit(solution)/shard_map/tmap/pallas_call | solution.py:110
  11.4 38.4 %first.1 = (f32[256,128]{1,0:T(8,128)S(1)}, bf16[2,4,4,128,128]{4,3,2,1,0:T(8,128)(2,1)S(1)}, bf16[2,4,4,128,128]{4,3,2,1,0:T(8,128)(2,1)S(1)}, f32[8,128]{1,0:T(8,128)S(1)}) custom-call(f32[2,4,4,64,256]{4,3,2,1,0:T(8,128)S(1)} %get-tuple-element.32.pa, f32[2,4,4,64,256]{4,3,2,1,0:T(8,128)S(1)} %get-tuple-element.33.pb, f32[256,128]{1,0:T(8,128)S(1)} %get-tuple-element.30.prior), custom_call_target="tpu_custom_call" | custom-call | tf_op jit(solution)/shard_map/first/pallas_call | solution.py:373
  49.9 3.8 %fmap.2 = bf16[32,64,128]{2,1,0:T(8,128)(2,1)S(1)} custom-call(s32[2,512]{1,0:T(2,128)S(1)} %sort.1.plan, bf16[320,64,256]{2,1,0:T(8,128)(2,1)S(1)} %bitcast.16, bf16[2,16,128,128]{3,2,1,0:T(8,128)(2,1)S(1)} %bitcast.21, bf16[2,16,128,128]{3,2,1,0:T(8,128)(2,1)S(1)} %bitcast.22), custom_call_target="tpu_custom_call" | custom-call | tf_op jit(solution)/shard_map/fmap/pallas_call | solution.py:128
  53.7 17.0 %cross.2 = (bf16[4,8,64,128]{3,2,1,0:T(8,128)(2,1)S(1)}, f32[8,128]{1,0:T(8,128)S(1)}, f32[8,128]{1,0:T(8,128)S(1)}) custom-call(bf16[4,8,64,128]{3,2,1,0:T(8,128)(2,1)S(1)} %bitcast.18, f32[8,64,128]{2,1,0:T(8,128)S(1)} %get-tuple-element.36.wgt, f32[8,128]{1,0:T(8,128)S(1)} %get-tuple-element.37.part), custom_call_target="tpu_custom_call" | custom-call | tf_op jit(solution)/shard_map/cross/pallas_call | solution.py:373
  70.7 4.4 %tmap.4 = (f32[2,4,4,64,256]{4,3,2,1,0:T(8,128)S(1)}, f32[2,4,4,64,256]{4,3,2,1,0:T(8,128)S(1)}) custom-call(s32[2,512]{1,0:T(2,128)S(1)} %sort.1.plan, bf16[320,64,256]{2,1,0:T(8,128)(2,1)S(1)} %bitcast.16, bf16[32,64,128]{2,1,0:T(8,128)(2,1)S(1)} %bitcast.24), custom_call_target="tpu_custom_call" | custom-call | tf_op jit(solution)/shard_map/tmap/pallas_call | solution.py:110
  75.1 40.8 %mid.1 = (f32[256,128]{1,0:T(8,128)S(1)}, f32[256,128]{1,0:T(8,128)S(1)}, f32[256,128]{1,0:T(8,128)S(1)}, f32[8,128]{1,0:T(8,128)S(1)}, bf16[2,4,4,128,128]{4,3,...) custom-call(f32[2,4,4,64,256]{4,3,2,1,0:T(8,128)S(1)} %get-tuple-element.39.pa, ...), custom_call_target="tpu_custom_call" | custom-call | tf_op jit(solution)/shard_map/mid/pallas_call | solution.py:373
  115.9 3.9 %fmap.3 = bf16[32,64,128]{2,1,0:T(8,128)(2,1)S(1)} custom-call(s32[2,512]{1,0:T(2,128)S(1)} %sort.1.plan, bf16[320,64,256]{2,1,0:T(8,128)(2,1)S(1)} %bitcast.16, bf16[2,16,128,128]{3,2,1,0:T(8,128)(2,1)S(1)} %bitcast.19, bf16[2,16,128,128]{3,2,1,0:T(8,128)(2,1)S(1)} %bitcast.20), custom_call_target="tpu_custom_call" | custom-call | tf_op jit(solution)/shard_map/fmap/pallas_call | solution.py:128
  119.8 16.0 %cross.3 = (bf16[4,8,64,128]{3,2,1,0:T(8,128)(2,1)S(1)}, f32[8,128]{1,0:T(8,128)S(1)}, f32[8,128]{1,0:T(8,128)S(1)}) custom-call(bf16[4,8,64,128]{3,2,1,0:T(8,128)(2,1)S(1)} %bitcast.17, f32[8,64,128]{2,1,0:T(8,128)S(1)} %get-tuple-element.36.wgt, f32[8,128]{1,0:T(8,128)S(1)} %get-tuple-element.47.part), custom_call_target="tpu_custom_call" | custom-call | tf_op jit(solution)/shard_map/cross/pallas_call | solution.py:373
  135.8 4.3 %tmap.5 = (bf16[2,4,4,64,256]{4,3,2,1,0:T(8,128)(2,1)S(1)}, bf16[2,4,4,64,256]{4,3,2,1,0:T(8,128)(2,1)S(1)}) custom-call(s32[2,512]{1,0:T(2,128)S(1)} %sort.1.plan, bf16[320,64,256]{2,1,0:T(8,128)(2,1)S(1)} %bitcast.16, bf16[32,64,128]{2,1,0:T(8,128)(2,1)S(1)} %bitcast.23), custom_call_target="tpu_custom_call" | custom-call | tf_op jit(solution)/shard_map/tmap/pallas_call | solution.py:110
  140.1 15.2 %last.1 = (f32[256,128]{1,0:T(8,128)S(1)}, f32[8,128]{1,0:T(8,128)S(1)}) custom-call(bf16[2,4,4,64,256]{4,3,2,1,0:T(8,128)(2,1)S(1)} %get-tuple-element.49.pa, bf16[2,4,4,64,256]{4,3,2,1,0:T(8,128)(2,1)S(1)} %get-tuple-element.50.pb, f32[8,128]{1,0:T(8,128)S(1)} %get-tuple-element.51.n1, f32[8,128]{1,0:T(8,128)S(1)} %get-tuple-element.52.dd, ...), custom_call_target="tpu_custom_call" | custom-call | tf_op jit(solution)/shard_map/last/pallas_call | solution.py:373
  155.3 0.8 subtract_bitcast_fusion
  (4 shorter events, 0.0 us)
Async XLA Ops:
  2.7 2.5 %slice-start = ((s8[10485760]{0:T(1024)(128)(4,1)}), s8[4194304]{0:T(1024)(128)(4,1)S(1)}, s32[]{:S(2)}) async-start(s8[10485760]{0:T(1024)(128)(4,1)} %bitcast.15), calls=%async_computation | async-start | bytes 8388608
  2.7 1.4 copy-start
  2.7 1.4 copy-start.1
  2.7 1.4 copy-start.2
  2.7 3.7 %slice-start.1 = ((s8[10485760]{0:T(1024)(128)(4,1)}), s8[4194304]{0:T(1024)(128)(4,1)S(1)}, s32[]{:S(2)}) async-start(s8[10485760]{0:T(1024)(128)(4,1)} %bitcast.15), calls=%async_computation.1 | async-start | bytes 8388608
  2.7 4.3 %slice-start.2 = ((s8[10485760]{0:T(1024)(128)(4,1)}), s8[2097152]{0:T(1024)(128)(4,1)S(1)}, s32[]{:S(2)}) async-start(s8[10485760]{0:T(1024)(128)(4,1)} %bitcast.15), calls=%async_computation.2 | async-start | bytes 4194304

commit v4 on v3

--- a/solution.py
+++ b/solution.py
@@ -282,12 +282,11 @@
     net.drain()
     assert (net.ns,net.nr)==FIRST_NET, (net.ns,net.nr)
 
-def mid_kernel(pa, pb, prior, r0, nrm, wi, r1, d1, it, nn, va, vb, dd, *s):
+def mid_kernel(pa, pb, prior, r0, nrm, wi, r1, it, va, vb, two, *s):
     sc=s[:-4]; sin,sout,ssem,rsem=s[-4:]
     y,z,c,r=place(); mate=dev(y,z,1-c,r)
-    ry=Ring(y,lambda i:dev(i,z,c,r)); rz=Ring(z,lambda i:dev(y,i,c,r)); rx=Ring(r,lambda i:dev(y,z,c,i))
-    here=rx.peers()+[mate]+[dev(y,z,1-c,x) for x in rx.to[1:]]
-    greet(here+ry.peers()+rz.peers())
+    ry=Ring(y,lambda i:dev(i,z,c,r)); rz=Ring(z,lambda i:dev(y,i,c,r))
+    greet([mate]+ry.peers()+rz.peers())
     net=Net(ssem,rsem)
     plane=[ry.peers(),rz.peers(),[mate]]
     ra=Reduce(net,sin,sout,plane,0)
@@ -299,27 +298,22 @@
     step=n0/(n0+ra.finish()[0:1])
     d0=r0[...]
     res=d0-step*(d0+prior[...]*t.T)
-    rb=Reduce(net,sin,sout,[here,ry.peers(),rz.peers()],7)
-    rb.start(rep(jnp.sum(res*res,axis=0,keepdims=True)))
-    it[...]=step*d0
-    r1[...]=res
-    n1=rb.finish()
-    nn[...]=n1
-    d=res+(n1[0:1]/n0)*d0
-    v=(prior[...]*d).astype(bf16)
+    v=(prior[...]*res).astype(bf16)
     va[c,z,y]=v[0:128]; vb[c,y,z]=v[128:256]
-    rc=Reduce(net,sin,sout,plane,20)
+    rc=Reduce(net,sin,sout,plane,7)
     def tick2(k):
         if k==0:
-            d1[...]=d
-            rc.start(rep(jnp.sum(d*d,axis=0,keepdims=True)))
+            it[...]=step*d0
+            r1[...]=res
+            first_row=lax.broadcasted_iota(jnp.int32,(8,128),0)==0
+            rc.start(jnp.where(first_row,rep(jnp.sum(res*res,axis=0,keepdims=True)),rep(jnp.sum(res*d0,axis=0,keepdims=True))))
         elif k>1: rc.step()
     gather_tiles(net,mate,c,ry,rz,va,vb,tick2)
-    dd[...]=rc.finish()
+    two[...]=rc.finish()
     net.drain()
     assert (net.ns,net.nr)==MID_NET, (net.ns,net.nr)
 
-def last_kernel(pa, pb, n1, dd, wi, back, step, *s):
+def last_kernel(pa, pb, top, low, wi, back, step, *s):
     sc=s[:-4]; sin,sout,ssem,rsem=s[-4:]
     y,z,c,r=place(); mate=dev(y,z,1-c,r)
     ry=Ring(y,lambda i:dev(i,z,c,r)); rz=Ring(z,lambda i:dev(y,i,c,r))
@@ -330,13 +324,13 @@
         if k==0: ra.start(wi[...])
         else: ra.step()
     t=reduce_tiles(net,mate,c,ry,rz,pa,pb,sc,tick)
-    step[...]=n1[...]/(dd[...]+ra.finish())
+    step[...]=top[...]/(low[...]+ra.finish())
     back[...]=t.T
     net.drain()
     assert (net.ns,net.nr)==LAST_NET, (net.ns,net.nr)
 
 CH=4
-def cross_kernel(img, wgt, part, w, tot, wi, g, sin, sout, ssem, rsem):
+def exchange(img, wgt, w, sin, sout, ssem, rsem, g, part, keep, base):
     y,z,c,r=place()
     rx=Ring(r,lambda i:dev(y,z,c,i))
     greet(rx.peers())
@@ -344,17 +338,19 @@
     n=8//CH
     B=[pl.ds(j*n,n) for j in range(CH)]
     s1=net.sender(g); k1=[net.taker() for j in range(CH)]
+    ra=Reduce(net,sin,sout,[rx.peers()],0)
+    ra.start(part)
     for j in range(CH):
         for d in FAR: net.put(img.at[rx.to[d],B[j]],g.at[d-1,B[j]],rx.dev[d],s1,k1[j])
-    ra=Reduce(net,sin,sout,[rx.peers()],0)
-    ra.start(part[...])
     sums=jnp.zeros((64,128),f32)
     s2=net.sender(g); k2=net.taker()
+    extra=base(ra.finish())
     for j in range(CH):
         b=B[j]
         x=img[r,b].astype(f32)
         net.take(k1[j],g.at[pl.ds(0,3),pl.ds(0,n)])
-        x=x+(g[0,b].astype(f32)+g[1,b].astype(f32)+g[2,b].astype(f32))
+        x=extra(b,x+(g[0,b].astype(f32)+g[1,b].astype(f32)+g[2,b].astype(f32)))
+        keep(b,x)
         m=wgt[b]*x
         w[r,b]=m.astype(bf16)
         s=w.at[r,b]
@@ -362,13 +358,30 @@
         sums=sums+jnp.sum(m*x,axis=0)
     rb=Reduce(net,sin,sout,[rx.peers()],3)
     rb.start(rep(jnp.sum(sums,axis=0,keepdims=True)))
-    tot[...]=ra.finish()
-    wi[...]=rb.finish()
+    wi=rb.finish()
     net.take(k2,g)
     net.drain()
     assert (net.ns,net.nr)==CROSS_NET, (net.ns,net.nr)
-
-FIRST_NET=(15,37); MID_NET=(21,43); LAST_NET=(9,21); CROSS_NET=(4,CH+3)
+    return wi
+
+def cross_kernel(img, wgt, part, w, tot, wi, image, g, sin, sout, ssem, rsem):
+    def base(total):
+        tot[...]=total
+        return lambda b,x: x
+    def keep(b,x): image[b]=x
+    wi[...]=exchange(img,wgt,w,sin,sout,ssem,rsem,g,part[...],keep,base)
+
+def again_kernel(img, wgt, part, n0, image, w, low, top, beta, wi, g, sin, sout, ssem, rsem):
+    def base(total):
+        n1=total[0:1]
+        ratio=n1/n0[0:1]
+        top[...]=rep(n1)
+        beta[...]=rep(ratio)
+        low[...]=rep(n1+ratio*(2.0*total[1:2]+ratio*n0[0:1]))
+        return lambda b,x: x+ratio*image[b]
+    wi[...]=exchange(img,wgt,w,sin,sout,ssem,rsem,g,part[...],lambda b,x:None,base)
+
+FIRST_NET=(15,37); MID_NET=(18,40); LAST_NET=(9,21); CROSS_NET=(4,CH+3)
 def _call(kernel, outs, scratch, cid, lim, name, *args):
     return pl.pallas_call(kernel,out_shape=outs,in_specs=[VM]*len(args),out_specs=tuple([VM]*len(outs)),
         scratch_shapes=scratch,compiler_params=pltpu.CompilerParams(collective_id=cid,has_side_effects=True,vmem_limit_bytes=lim<<20),name=name)(*args)
@@ -377,11 +390,13 @@
 def first(pa,pb,prior):
     return _call(first_kernel,[TILE,VA,VA,ROW],reduce_scratch(f32,f32)+tail(7,FIRST_NET),0,22,"first",pa,pb,prior)
 def mid(pa,pb,prior,r0,nrm,wi):
-    return _call(mid_kernel,[TILE,TILE,TILE,ROW,VA,VA,ROW],reduce_scratch(bf16,pa.dtype)+tail(27,MID_NET),1,18,"mid",pa,pb,prior,r0,nrm,wi)
-def last(pa,pb,n1,dd,wi):
-    return _call(last_kernel,[TILE,ROW],reduce_scratch(bf16,pa.dtype)+tail(7,LAST_NET),2,14,"last",pa,pb,n1,dd,wi)
+    return _call(mid_kernel,[TILE,TILE,VA,VA,ROW],reduce_scratch(bf16,pa.dtype)+tail(14,MID_NET),1,18,"mid",pa,pb,prior,r0,nrm,wi)
+def last(pa,pb,top,low,wi):
+    return _call(last_kernel,[TILE,ROW],reduce_scratch(bf16,pa.dtype)+tail(7,LAST_NET),2,14,"last",pa,pb,top,low,wi)
 def cross(img,wgt,part):
-    return _call(cross_kernel,[SH((4,8,64,128),bf16),ROW,ROW],[pltpu.VMEM((3,8,64,128),bf16)]+tail(6,CROSS_NET),3,8,"cross",img.reshape(4,8,64,128),wgt,part)
+    return _call(cross_kernel,[SH((4,8,64,128),bf16),ROW,ROW,SH((8,64,128))],[pltpu.VMEM((3,8,64,128),bf16)]+tail(6,CROSS_NET),3,8,"cross",img.reshape(4,8,64,128),wgt,part)
+def again(img,wgt,part,n0,image):
+    return _call(again_kernel,[SH((4,8,64,128),bf16),ROW,ROW,ROW,ROW],[pltpu.VMEM((3,8,64,128),bf16)]+tail(6,CROSS_NET),4,8,"again",img.reshape(4,8,64,128),wgt,part,n0,image)
 
 def per_device(footprints, block_sounding, block_tile, block_count, observations, obs_weight, prior_std):
     F = footprints
@@ -389,14 +404,15 @@
     pa, pb = transpose_map(plan, F, w0, f32)
     r0, va, vb, norm = first(pa, pb, prior)
     img = forward_map(plan, F, va, vb)
-    w, norm, wi = cross(img, wgt, norm)
+    w, norm, wi, image = cross(img, wgt, norm)
     pa, pb = transpose_map(plan, F, w.reshape(32, 64, 128), f32)
-    r1, d1, it, n1, va, vb, dd = mid(pa, pb, prior, r0, norm, wi)
+    r1, it, va, vb, two = mid(pa, pb, prior, r0, norm, wi)
     img = forward_map(plan, F, va, vb)
-    w, dd, wi = cross(img, wgt, dd)
+    w, low, top, beta, wi = again(img, wgt, two, norm, image)
     pa, pb = transpose_map(plan, F, w.reshape(32, 64, 128), bf16)
-    back, step = last(pa, pb, n1, dd, wi)
-    step = step[0:1]
+    back, step = last(pa, pb, top, low, wi)
+    step, beta = step[0:1], beta[0:1]
+    d1 = r1 + beta * r0
     resid = r1 - step * (d1 + prior * back)
     flux = prior * (it + step * d1)
     return flux[None, None], resid[None, None]

time: 156 us -> 145 us (0.929)
  Pallas kernels: 149 us -> 139 us
    pallas_call x5, Pallas kernels: 127 us -> 112 us  [_call(): pl.pallas_call(kernel, out_shape=outs, in_specs=[VM] * len(args), out_spe...]
    pallas_call x3, Pallas kernels: 13.1 us -> 15.9 us  [transpose_map(): pl.pallas_call(t_kernel, out_shape=(o, o), in_specs=[SM, VM, VM], out_spe...]
    pallas_call x2, Pallas kernels: 7.7 us -> 9.77 us  [forward_map(): pl.pallas_call(f_kernel, out_shape=SH((32, 64, 128), bf16), in_specs=[SM,...]
where the time goes in v4:
time: 145 us; the launch traced here: 146 us
  Pallas kernels  139 us (96%)
  local copies, waits for them, and re-layouts  4.4 us (3%)
    pallas_call x5, Pallas kernels, _call(): pl.pallas_call(kernel, out_shape=outs, in_specs=[VM] * len(args), out_spe...  112 us
    pallas_call x3, Pallas kernels, transpose_map(): pl.pallas_call(t_kernel, out_shape=(o, o), in_specs=[SM, VM, VM], out_spe...  15.9 us
    pallas_call x2, Pallas kernels, forward_map(): pl.pallas_call(f_kernel, out_shape=SH((32, 64, 128), bf16), in_specs=[SM,...  9.77 us
    unnamed x12, local copies, waits for them, and re-layouts  3.02 us

profile of v4, /device:TPU:1, one launch (start us, length us, event | category | flops | bytes accessed | tf_op | source)
XLA Modules:
  0.0 145.5 jit_solution(973039214412325182)
XLA Ops:
  1.3 0.7 stack.10
  2.0 0.7 stack.9
  2.7 0.0 slice-start
  2.7 0.0 copy-start
  2.7 0.0 copy-start.1
  2.7 0.0 copy-start.2
  2.7 0.0 slice-start.1
  2.7 0.0 slice-start.2
  2.7 0.6 sort.1.plan
  3.3 0.8 copy-done
  4.1 0.0 copy-done.1
  4.1 0.0 copy-done.2
  4.1 0.8 spread.1
  4.8 0.4 slice-done
  5.2 1.3 slice-done.1
  6.5 0.6 slice-done.2
  7.1 5.3 %tmap.3 = (f32[2,4,4,64,256]{4,3,2,1,0:T(8,128)S(1)}, f32[2,4,4,64,256]{4,3,2,1,0:T(8,128)S(1)}) custom-call(s32[2,512]{1,0:T(2,128)S(1)} %sort.1.plan, bf16[320,64,256]{2,1,0:T(8,128)(2,1)S(1)} %bitcast.18, bf16[32,64,128]{2,1,0:T(8,128)(2,1)S(1)} %get-tuple-element.32.w), custom_call_target="tpu_custom_call" | custom-call | tf_op jit(solution)/shard_map/tmap/pallas_call | solution.py:110
  12.4 37.7 %first.1 = (f32[256,128]{1,0:T(8,128)S(1)}, bf16[2,4,4,128,128]{4,3,2,1,0:T(8,128)(2,1)S(1)}, bf16[2,4,4,128,128]{4,3,2,1,0:T(8,128)(2,1)S(1)}, f32[8,128]{1,0:T(8,128)S(1)}) custom-call(f32[2,4,4,64,256]{4,3,2,1,0:T(8,128)S(1)} %get-tuple-element.33.pa, f32[2,4,4,64,256]{4,3,2,1,0:T(8,128)S(1)} %get-tuple-element.34.pb, f32[256,128]{1,0:T(8,128)S(1)} %get-tuple-element.31.prior), custom_call_target="tpu_custom_call" | custom-call | tf_op jit(solution)/shard_map/first/pallas_call | solution.py:386
  50.1 4.9 %fmap.2 = bf16[32,64,128]{2,1,0:T(8,128)(2,1)S(1)} custom-call(s32[2,512]{1,0:T(2,128)S(1)} %sort.1.plan, bf16[320,64,256]{2,1,0:T(8,128)(2,1)S(1)} %bitcast.18, bf16[2,16,128,128]{3,2,1,0:T(8,128)(2,1)S(1)} %bitcast.23, bf16[2,16,128,128]{3,2,1,0:T(8,128)(2,1)S(1)} %bitcast.24), custom_call_target="tpu_custom_call" | custom-call | tf_op jit(solution)/shard_map/fmap/pallas_call | solution.py:128
  55.0 16.3 %cross.1 = (bf16[4,8,64,128]{3,2,1,0:T(8,128)(2,1)S(1)}, f32[8,128]{1,0:T(8,128)S(1)}, f32[8,128]{1,0:T(8,128)S(1)}, f32[8,64,128]{2,1,0:T(8,128)S(1)}) custom-call(bf16[4,8,64,128]{3,2,1,0:T(8,128)(2,1)S(1)} %bitcast.20, f32[8,64,128]{2,1,0:T(8,128)S(1)} %get-tuple-element.37.wgt, f32[8,128]{1,0:T(8,128)S(1)} %get-tuple-element.38.part), custom_call_target="tpu_custom_call" | custom-call | tf_op jit(solution)/shard_map/cross/pallas_call | solution.py:386
  71.3 5.3 %tmap.4 = (f32[2,4,4,64,256]{4,3,2,1,0:T(8,128)S(1)}, f32[2,4,4,64,256]{4,3,2,1,0:T(8,128)S(1)}) custom-call(s32[2,512]{1,0:T(2,128)S(1)} %sort.1.plan, bf16[320,64,256]{2,1,0:T(8,128)(2,1)S(1)} %bitcast.18, bf16[32,64,128]{2,1,0:T(8,128)(2,1)S(1)} %bitcast.26), custom_call_target="tpu_custom_call" | custom-call | tf_op jit(solution)/shard_map/tmap/pallas_call | solution.py:110
  76.6 27.8 %mid.1 = (f32[256,128]{1,0:T(8,128)S(1)}, f32[256,128]{1,0:T(8,128)S(1)}, bf16[2,4,4,128,128]{4,3,2,1,0:T(8,128)(2,1)S(1)}, bf16[2,4,4,128,128]{4,3,2,1,0:T(8,128)(2,1)S(1)}, f32[8,128]{1,0:T(8,128)S(1)}) custom-call(f32[2,4,4,64,256]{4,3,2,1,0:T(8,128)S(1)} %get-tuple-element.40.pa, f32[2,4,4,64,256]{4,3,2,1,0:T(8,128)S(1)} %get-tuple-element.41.pb, ...), custom_call_target="tpu_custom_call" | custom-call | tf_op jit(solution)/shard_map/mid/pallas_call | solution.py:386
  104.5 4.9 %fmap.3 = bf16[32,64,128]{2,1,0:T(8,128)(2,1)S(1)} custom-call(s32[2,512]{1,0:T(2,128)S(1)} %sort.1.plan, bf16[320,64,256]{2,1,0:T(8,128)(2,1)S(1)} %bitcast.18, bf16[2,16,128,128]{3,2,1,0:T(8,128)(2,1)S(1)} %bitcast.21, bf16[2,16,128,128]{3,2,1,0:T(8,128)(2,1)S(1)} %bitcast.22), custom_call_target="tpu_custom_call" | custom-call | tf_op jit(solution)/shard_map/fmap/pallas_call | solution.py:128
  109.4 16.6 %again.1 = (bf16[4,8,64,128]{3,2,1,0:T(8,128)(2,1)S(1)}, f32[8,128]{1,0:T(8,128)S(1)}, f32[8,128]{1,0:T(8,128)S(1)}, f32[8,128]{1,0:T(8,128)S(1)}, f32[8,128]{1,0:T(8,128)S(1)}) custom-call(bf16[4,8,64,128]{3,2,1,0:T(8,128)(2,1)S(1)} %bitcast.19, f32[8,64,128]{2,1,0:T(8,128)S(1)} %get-tuple-element.37.wgt, f32[8,128]{1,0:T(8,128)S(1)} %get-tuple-element.48.part, ...), custom_call_target="tpu_custom_call" | custom-call | tf_op jit(solution)/shard_map/again/pallas_call | solution.py:386
  126.0 5.2 %tmap.5 = (bf16[2,4,4,64,256]{4,3,2,1,0:T(8,128)(2,1)S(1)}, bf16[2,4,4,64,256]{4,3,2,1,0:T(8,128)(2,1)S(1)}) custom-call(s32[2,512]{1,0:T(2,128)S(1)} %sort.1.plan, bf16[320,64,256]{2,1,0:T(8,128)(2,1)S(1)} %bitcast.18, bf16[32,64,128]{2,1,0:T(8,128)(2,1)S(1)} %bitcast.25), custom_call_target="tpu_custom_call" | custom-call | tf_op jit(solution)/shard_map/tmap/pallas_call | solution.py:110
  131.2 13.5 %last.1 = (f32[256,128]{1,0:T(8,128)S(1)}, f32[8,128]{1,0:T(8,128)S(1)}) custom-call(bf16[2,4,4,64,256]{4,3,2,1,0:T(8,128)(2,1)S(1)} %get-tuple-element.51.pa, bf16[2,4,4,64,256]{4,3,2,1,0:T(8,128)(2,1)S(1)} %get-tuple-element.52.pb, f32[8,128]{1,0:T(8,128)S(1)} %get-tuple-element.53.top, f32[8,128]{1,0:T(8,128)S(1)} %get-tuple-element.54.low, ...), custom_call_target="tpu_custom_call" | custom-call | tf_op jit(solution)/shard_map/last/pallas_call | solution.py:386
  144.8 0.8 subtract_bitcast_fusion
  (4 shorter events, 0.0 us)
Async XLA Ops:
  2.7 2.5 %slice-start = ((s8[10485760]{0:T(1024)(128)(4,1)}), s8[4194304]{0:T(1024)(128)(4,1)S(1)}, s32[]{:S(2)}) async-start(s8[10485760]{0:T(1024)(128)(4,1)} %bitcast.17), calls=%async_computation | async-start | bytes 8388608
  2.7 1.4 copy-start
  2.7 1.4 copy-start.1
  2.7 1.4 copy-start.2
  2.7 3.7 %slice-start.1 = ((s8[10485760]{0:T(1024)(128)(4,1)}), s8[4194304]{0:T(1024)(128)(4,1)S(1)}, s32[]{:S(2)}) async-start(s8[10485760]{0:T(1024)(128)(4,1)} %bitcast.17), calls=%async_computation.1 | async-start | bytes 8388608
  2.7 4.3 %slice-start.2 = ((s8[10485760]{0:T(1024)(128)(4,1)}), s8[2097152]{0:T(1024)(128)(4,1)S(1)}, s32[]{:S(2)}) async-start(s8[10485760]{0:T(1024)(128)(4,1)} %bitcast.17), calls=%async_computation.2 | async-start | bytes 4194304

commit v5 on v4

--- a/solution.py
+++ b/solution.py
@@ -34,8 +34,9 @@
 
 def sort_kernel(cnt, packed, plan):
     p=packed[...].astype(f32)
-    q=p.T
-    slots,gt=sort_blocks(cnt[0],p[0:1],q[:,0:1],q[:,1:2])
+    q=p.T[:,0:1]
+    tile=jnp.floor(q*(1.0/64.0))
+    slots,gt=sort_blocks(cnt[0],jnp.floor(p[0:1]*(1.0/64.0)),tile,q-64.0*tile)
     plan[0:1]=slots.astype(jnp.int32)
     plan[1:2,0:128]=gt.astype(jnp.int32)
 
@@ -52,7 +53,7 @@
 
 SM=pl.BlockSpec(memory_space=pltpu.SMEM); VM=pl.BlockSpec(memory_space=pltpu.VMEM)
 def begin(cnt, bs, bt, obs, weight, prior):
-    packed=jnp.pad(jnp.stack([bt,bs]),((0,6),(0,NBP-NB)))
+    packed=jnp.pad((bt*64+bs).reshape(1,NB),((0,7),(0,NBP-NB)))
     plan=pl.pallas_call(sort_kernel,out_shape=SH((2,NSLOT),jnp.int32),in_specs=[SM,VM],out_specs=VM,
         cost_estimate=pl.CostEstimate(flops=10**10,bytes_accessed=3*10**7,transcendentals=0),
         compiler_params=pltpu.CompilerParams(vmem_limit_bytes=8<<20),name="sort")(cnt,packed)
@@ -166,29 +167,44 @@
     def peers(self): return self.dev[1:4]
 FAR=(1,3,2)
 
-def reduce_scratch(dt, cdt):
+def reduce_scratch(dt, cdt, relays=0):
     V=pltpu.VMEM
-    return [V((4,4,64,256),cdt)]*2+[V((4,4,64,256),dt)]*2+[V((3,4,64,256),dt)]*2+[V((3,64,256),dt)]*4
-
-def reduce_tiles(net, mate, c, ry, rz, pa, pb, sc, tick=lambda k:None):
-    ra,rb,qa,qb,ga,gb,sa,sb,ha,hb=sc
+    return [V((4,4,64,256),cdt)]*2+[V((4,4,64,256),dt)]*2+[V((3,4,64,256),dt)]*2+[V((3,64,256),dt)]*4+[V((relays,64,256),dt)]*(4 if relays else 0)
+
+def reduce_tiles(net, mate, c, ry, rz, pa, pb, sc, tick=lambda k:None, relays=0):
+    ra,rb,qa,qb,ga,gb,sa,sb,ha,hb=sc[:10]
+    ia,ib,oa,ob=sc[10:] if relays else (None,)*4
     sides=((ry,rz,pa,ra,qa,ga,sa,ha),(rz,ry,pb,rb,qb,gb,sb,hb))
+    inn=(ia,ib); out=(oa,ob)
     order=(2,1,3,0)
+    way=lambda k: 1 if k%2==0 else 3
     s0=[net.sender(r) for (m,n,p,r,q,g,s,h) in sides]
     k0=[[net.taker() for x in sides] for e in order]
     for k,e in enumerate(order):
         for b,(m,n,p,r,q,g,s,h) in enumerate(sides):
             net.put(p.at[1-c,n.to[e]],r.at[n.to[e]],mate,s0[b],k0[k][b])
     tick(0)
-    s1=[net.sender(g) for (m,n,p,r,q,g,s,h) in sides]
+    if relays<4: s1=[net.sender(g.at[pl.ds(0,3),pl.ds(0,4-relays)]) for (m,n,p,r,q,g,s,h) in sides]
     k1=[[net.taker() for x in sides] for e in order]
+    if relays:
+        sr=[net.sender(x) for x in inn]
+        sn=[net.sender(g.at[pl.ds(0,2),pl.ds(0,relays)]) for (m,n,p,r,q,g,s,h) in sides]
+        kr=[[net.taker() for x in sides] for k in range(relays)]
     for k,e in enumerate(order):
         for b,(m,n,p,r,q,g,s,h) in enumerate(sides):
             j=n.to[e]
             net.take(k0[k][b],r.at[j])
-            for d in FAR:
+            for d in (2,4-way(k),way(k)) if k<relays else FAR:
                 q[j,m.to[d]]=(p[c,j,m.to[d]].astype(f32)+r[j,m.to[d]].astype(f32)).astype(q.dtype)
-                net.put(q.at[j,m.to[d]],g.at[d-1,j],m.dev[d],s1[b],k1[k][b])
+                if k>=relays: net.put(q.at[j,m.to[d]],g.at[d-1,j],m.dev[d],s1[b],k1[k][b])
+                elif d==2: net.put(q.at[j,m.to[d]],inn[b].at[k],m.dev[way(k)],sr[b],kr[k][b])
+                elif d!=way(k): net.put(q.at[j,m.to[d]],g.at[d-1,j],m.dev[d],sn[b],k1[k][b])
+    for k in range(relays):
+        for b,(m,n,p,r,q,g,s,h) in enumerate(sides):
+            j=n.to[order[k]]; w=way(k)
+            net.take(kr[k][b],inn[b].at[k])
+            out[b][k]=(q[j,m.to[w]].astype(f32)+inn[b][k].astype(f32)).astype(q.dtype)
+            net.put(out[b].at[k],g.at[w-1,j],m.dev[w],sn[b],k1[k][b])
     tick(1)
     s2=[net.sender(s) for (m,n,p,r,q,g,s,h) in sides]
     k2=[net.taker() for x in sides]
@@ -197,8 +213,12 @@
         for b,(m,n,p,r,q,g,s,h) in enumerate(sides):
             j=n.to[e]
             x=p[c,j,m.i].astype(f32)+r[j,m.i].astype(f32)
-            net.take(k1[k][b],h)
-            x=x+(g[0,j].astype(f32)+g[1,j].astype(f32)+g[2,j].astype(f32))
+            if k<relays:
+                net.take(k1[k][b],h.at[pl.ds(0,2)])
+                x=x+(g[0,j].astype(f32)+g[2,j].astype(f32))
+            else:
+                net.take(k1[k][b],h)
+                x=x+(g[0,j].astype(f32)+g[1,j].astype(f32)+g[2,j].astype(f32))
             if e:
                 s[e-1]=x.astype(s.dtype)
                 net.put(s.at[e-1],h.at[e-1],n.dev[e],s2[b],k2[b])
@@ -267,7 +287,7 @@
     ry=Ring(y,lambda i:dev(i,z,c,r)); rz=Ring(z,lambda i:dev(y,i,c,r))
     greet([mate]+ry.peers()+rz.peers())
     net=Net(ssem,rsem)
-    t=reduce_tiles(net,mate,c,ry,rz,pa,pb,sc)
+    t=reduce_tiles(net,mate,c,ry,rz,pa,pb,sc,relays=RELAYS)
     res=prior[...]*t.T
     v=(prior[...]*res).astype(bf16)
     va[c,z,y]=v[0:128]; vb[c,y,z]=v[128:256]
@@ -381,14 +401,14 @@
         return lambda b,x: x+ratio*image[b]
     wi[...]=exchange(img,wgt,w,sin,sout,ssem,rsem,g,part[...],lambda b,x:None,base)
 
-FIRST_NET=(15,37); MID_NET=(18,40); LAST_NET=(9,21); CROSS_NET=(4,CH+3)
+RELAYS=4; FIRST_NET=(17,45); MID_NET=(18,40); LAST_NET=(9,21); CROSS_NET=(4,CH+3)
 def _call(kernel, outs, scratch, cid, lim, name, *args):
     return pl.pallas_call(kernel,out_shape=outs,in_specs=[VM]*len(args),out_specs=tuple([VM]*len(outs)),
         scratch_shapes=scratch,compiler_params=pltpu.CompilerParams(collective_id=cid,has_side_effects=True,vmem_limit_bytes=lim<<20),name=name)(*args)
 VA=SH((2,4,4,128,128),bf16); ROW=SH((8,128)); TILE=SH((256,128))
 def tail(n, net): return [pltpu.VMEM((n,8,128),f32)]*2+[pltpu.SemaphoreType.DMA((k,)) for k in net]
 def first(pa,pb,prior):
-    return _call(first_kernel,[TILE,VA,VA,ROW],reduce_scratch(f32,f32)+tail(7,FIRST_NET),0,22,"first",pa,pb,prior)
+    return _call(first_kernel,[TILE,VA,VA,ROW],reduce_scratch(f32,f32,RELAYS)+tail(7,FIRST_NET),0,22,"first",pa,pb,prior)
 def mid(pa,pb,prior,r0,nrm,wi):
     return _call(mid_kernel,[TILE,TILE,VA,VA,ROW],reduce_scratch(bf16,pa.dtype)+tail(14,MID_NET),1,18,"mid",pa,pb,prior,r0,nrm,wi)
 def last(pa,pb,top,low,wi):

time: 145 us -> 142 us (0.979)
  Pallas kernels: 139 us -> 136 us
    pallas_call x5, Pallas kernels: 112 us -> 119 us  [_call(): pl.pallas_call(kernel, out_shape=outs, in_specs=[VM] * len(args), out_spe...]
    pallas_call x3, Pallas kernels: 15.9 us -> 10.3 us  [transpose_map(): pl.pallas_call(t_kernel, out_shape=(o, o), in_specs=[SM, VM, VM], out_spe...]
    pallas_call x2, Pallas kernels: 9.77 us -> 5.62 us  [forward_map(): pl.pallas_call(f_kernel, out_shape=SH((32, 64, 128), bf16), in_specs=[SM,...]
where the time goes in v5:
time: 142 us
  Pallas kernels  136 us (96%)
  local copies, waits for them, and re-layouts  3.07 us (2%)
  other arithmetic  1.46 us (1%)
  between operations  1.42 us (1%)
    pallas_call x5, Pallas kernels, _call(): pl.pallas_call(kernel, out_shape=outs, in_specs=[VM] * len(args), out_spe...  119 us
    pallas_call x3, Pallas kernels, transpose_map(): pl.pallas_call(t_kernel, out_shape=(o, o), in_specs=[SM, VM, VM], out_spe...  10.3 us
    pallas_call x2, Pallas kernels, forward_map(): pl.pallas_call(f_kernel, out_shape=SH((32, 64, 128), bf16), in_specs=[SM,...  5.62 us
    unnamed x12, local copies, waits for them, and re-layouts  3.06 us

profile of v5, /device:TPU:1, one launch (start us, length us, event | category | flops | bytes accessed | tf_op | source)
XLA Modules:
  0.0 142.0 jit_solution(3392903517270237735)
XLA Ops:
  1.3 0.7 multiply_add_fusion.1
  2.0 0.0 slice-start
  2.0 0.0 copy-start
  2.0 0.0 copy-start.1
  2.0 0.0 copy-start.2
  2.0 0.0 slice-start.1
  2.0 0.0 slice-start.2
  2.1 0.5 sort.1.plan
  2.6 0.8 copy-done
  3.4 0.0 copy-done.1
  3.4 0.0 copy-done.2
  3.4 0.8 spread.1
  4.1 0.4 slice-done
  4.5 1.3 slice-done.1
  5.8 0.6 slice-done.2
  6.4 3.5 %tmap.3 = (f32[2,4,4,64,256]{4,3,2,1,0:T(8,128)S(1)}, f32[2,4,4,64,256]{4,3,2,1,0:T(8,128)S(1)}) custom-call(s32[2,512]{1,0:T(2,128)S(1)} %sort.1.plan, bf16[320,64,256]{2,1,0:T(8,128)(2,1)S(1)} %bitcast.18, bf16[32,64,128]{2,1,0:T(8,128)(2,1)S(1)} %get-tuple-element.32.w), custom_call_target="tpu_custom_call" | custom-call | tf_op jit(solution)/shard_map/tmap/pallas_call | solution.py:111
  9.8 38.4 %first.1 = (f32[256,128]{1,0:T(8,128)S(1)}, bf16[2,4,4,128,128]{4,3,2,1,0:T(8,128)(2,1)S(1)}, bf16[2,4,4,128,128]{4,3,2,1,0:T(8,128)(2,1)S(1)}, f32[8,128]{1,0:T(8,128)S(1)}) custom-call(f32[2,4,4,64,256]{4,3,2,1,0:T(8,128)S(1)} %get-tuple-element.33.pa, f32[2,4,4,64,256]{4,3,2,1,0:T(8,128)S(1)} %get-tuple-element.34.pb, f32[256,128]{1,0:T(8,128)S(1)} %get-tuple-element.31.prior), custom_call_target="tpu_custom_call" | custom-call | tf_op jit(solution)/shard_map/first/pallas_call | solution.py:406
  48.2 2.8 %fmap.2 = bf16[32,64,128]{2,1,0:T(8,128)(2,1)S(1)} custom-call(s32[2,512]{1,0:T(2,128)S(1)} %sort.1.plan, bf16[320,64,256]{2,1,0:T(8,128)(2,1)S(1)} %bitcast.18, bf16[2,16,128,128]{3,2,1,0:T(8,128)(2,1)S(1)} %bitcast.23, bf16[2,16,128,128]{3,2,1,0:T(8,128)(2,1)S(1)} %bitcast.24), custom_call_target="tpu_custom_call" | custom-call | tf_op jit(solution)/shard_map/fmap/pallas_call | solution.py:129
  51.0 17.4 %cross.1 = (bf16[4,8,64,128]{3,2,1,0:T(8,128)(2,1)S(1)}, f32[8,128]{1,0:T(8,128)S(1)}, f32[8,128]{1,0:T(8,128)S(1)}, f32[8,64,128]{2,1,0:T(8,128)S(1)}) custom-call(bf16[4,8,64,128]{3,2,1,0:T(8,128)(2,1)S(1)} %bitcast.20, f32[8,64,128]{2,1,0:T(8,128)S(1)} %get-tuple-element.37.wgt, f32[8,128]{1,0:T(8,128)S(1)} %get-tuple-element.38.part), custom_call_target="tpu_custom_call" | custom-call | tf_op jit(solution)/shard_map/cross/pallas_call | solution.py:406
  68.5 3.5 %tmap.4 = (f32[2,4,4,64,256]{4,3,2,1,0:T(8,128)S(1)}, f32[2,4,4,64,256]{4,3,2,1,0:T(8,128)S(1)}) custom-call(s32[2,512]{1,0:T(2,128)S(1)} %sort.1.plan, bf16[320,64,256]{2,1,0:T(8,128)(2,1)S(1)} %bitcast.18, bf16[32,64,128]{2,1,0:T(8,128)(2,1)S(1)} %bitcast.26), custom_call_target="tpu_custom_call" | custom-call | tf_op jit(solution)/shard_map/tmap/pallas_call | solution.py:111
  72.0 29.2 %mid.1 = (f32[256,128]{1,0:T(8,128)S(1)}, f32[256,128]{1,0:T(8,128)S(1)}, bf16[2,4,4,128,128]{4,3,2,1,0:T(8,128)(2,1)S(1)}, bf16[2,4,4,128,128]{4,3,2,1,0:T(8,128)(2,1)S(1)}, f32[8,128]{1,0:T(8,128)S(1)}) custom-call(f32[2,4,4,64,256]{4,3,2,1,0:T(8,128)S(1)} %get-tuple-element.40.pa, f32[2,4,4,64,256]{4,3,2,1,0:T(8,128)S(1)} %get-tuple-element.41.pb, ...), custom_call_target="tpu_custom_call" | custom-call | tf_op jit(solution)/shard_map/mid/pallas_call | solution.py:406
  101.1 2.8 %fmap.3 = bf16[32,64,128]{2,1,0:T(8,128)(2,1)S(1)} custom-call(s32[2,512]{1,0:T(2,128)S(1)} %sort.1.plan, bf16[320,64,256]{2,1,0:T(8,128)(2,1)S(1)} %bitcast.18, bf16[2,16,128,128]{3,2,1,0:T(8,128)(2,1)S(1)} %bitcast.21, bf16[2,16,128,128]{3,2,1,0:T(8,128)(2,1)S(1)} %bitcast.22), custom_call_target="tpu_custom_call" | custom-call | tf_op jit(solution)/shard_map/fmap/pallas_call | solution.py:129
  103.9 18.4 %again.1 = (bf16[4,8,64,128]{3,2,1,0:T(8,128)(2,1)S(1)}, f32[8,128]{1,0:T(8,128)S(1)}, f32[8,128]{1,0:T(8,128)S(1)}, f32[8,128]{1,0:T(8,128)S(1)}, f32[8,128]{1,0:T(8,128)S(1)}) custom-call(bf16[4,8,64,128]{3,2,1,0:T(8,128)(2,1)S(1)} %bitcast.19, f32[8,64,128]{2,1,0:T(8,128)S(1)} %get-tuple-element.37.wgt, f32[8,128]{1,0:T(8,128)S(1)} %get-tuple-element.48.part, ...), custom_call_target="tpu_custom_call" | custom-call | tf_op jit(solution)/shard_map/again/pallas_call | solution.py:406
  122.3 3.4 %tmap.5 = (bf16[2,4,4,64,256]{4,3,2,1,0:T(8,128)(2,1)S(1)}, bf16[2,4,4,64,256]{4,3,2,1,0:T(8,128)(2,1)S(1)}) custom-call(s32[2,512]{1,0:T(2,128)S(1)} %sort.1.plan, bf16[320,64,256]{2,1,0:T(8,128)(2,1)S(1)} %bitcast.18, bf16[32,64,128]{2,1,0:T(8,128)(2,1)S(1)} %bitcast.25), custom_call_target="tpu_custom_call" | custom-call | tf_op jit(solution)/shard_map/tmap/pallas_call | solution.py:111
  125.7 15.5 %last.1 = (f32[256,128]{1,0:T(8,128)S(1)}, f32[8,128]{1,0:T(8,128)S(1)}) custom-call(bf16[2,4,4,64,256]{4,3,2,1,0:T(8,128)(2,1)S(1)} %get-tuple-element.51.pa, bf16[2,4,4,64,256]{4,3,2,1,0:T(8,128)(2,1)S(1)} %get-tuple-element.52.pb, f32[8,128]{1,0:T(8,128)S(1)} %get-tuple-element.53.top, f32[8,128]{1,0:T(8,128)S(1)} %get-tuple-element.54.low, ...), custom_call_target="tpu_custom_call" | custom-call | tf_op jit(solution)/shard_map/last/pallas_call | solution.py:406
  141.3 0.8 subtract_bitcast_fusion
  (4 shorter events, 0.0 us)
Async XLA Ops:
  2.0 2.5 %slice-start = ((s8[10485760]{0:T(1024)(128)(4,1)}), s8[4194304]{0:T(1024)(128)(4,1)S(1)}, s32[]{:S(2)}) async-start(s8[10485760]{0:T(1024)(128)(4,1)} %bitcast.17), calls=%async_computation | async-start | bytes 8388608
  2.0 1.4 copy-start
  2.0 1.4 copy-start.1
  2.0 1.4 copy-start.2
  2.0 3.8 %slice-start.1 = ((s8[10485760]{0:T(1024)(128)(4,1)}), s8[4194304]{0:T(1024)(128)(4,1)S(1)}, s32[]{:S(2)}) async-start(s8[10485760]{0:T(1024)(128)(4,1)} %bitcast.17), calls=%async_computation.1 | async-start | bytes 8388608
  2.0 4.3 %slice-start.2 = ((s8[10485760]{0:T(1024)(128)(4,1)}), s8[2097152]{0:T(1024)(128)(4,1)S(1)}, s32[]{:S(2)}) async-start(s8[10485760]{0:T(1024)(128)(4,1)} %bitcast.17), calls=%async_computation.2 | async-start | bytes 4194304

commit v6 on v5

--- a/solution.py
+++ b/solution.py
@@ -79,7 +79,7 @@
         out.append(F[lax.shift_right_logical(jnp.maximum(v-1,0),6)])
     return jnp.concatenate(out,axis=0)
 
-def t_kernel(plan, F, w, pa, pb, acc, wt0, wt1):
+def t_kernel(plan, F, w, pa, pb, wt0, wt1, *rest):
     lane=lax.broadcasted_iota(jnp.int32,(128,128),1)
     for p in range(16):
         x=jnp.concatenate([w[2*p],w[2*p+1]],axis=0).astype(f32).T
@@ -92,24 +92,32 @@
         wt1[2*p+1]=jnp.where(lo,z,x).astype(bf16)
     wt0[32]=jnp.zeros((128,128),bf16)
     wt1[32]=jnp.zeros((128,128),bf16)
-    acc[...]=jnp.zeros_like(acc)
+    direct=pa.dtype==f32
+    for ref in (pa,pb) if direct else rest: ref[...]=jnp.zeros_like(ref)
     def body(i):
         for j in range(UN):
             g=i*UN+j
             s=[snd(plan,g,k) for k in range(4)]
             lhs=jnp.concatenate([wt0[s[0]]+wt1[s[1]],wt0[s[2]]+wt1[s[3]]],axis=1)
-            acc[plan[1,g]]+=jnp.dot(lhs,four(plan,F,g),preferred_element_type=f32)
+            x=jnp.dot(lhs,four(plan,F,g),preferred_element_type=f32)
+            t=jnp.minimum(plan[1,g],31)
+            if direct:
+                c=jnp.bitwise_and(t,1); z=jnp.bitwise_and(lax.shift_right_logical(t,1),3); y=lax.shift_right_logical(t,3)
+                pa[c,z,y]+=x[0:64]
+                pb[c,y,z]+=x[64:128]
+            else: rest[0][t]+=x
     group_loop(plan,body)
-    for y in range(4):
-        for z in range(4):
-            for c in range(2):
-                x=acc[(y*4+z)*2+c].astype(pa.dtype)
-                pa[c,z,y]=x[0:64]
-                pb[c,y,z]=x[64:128]
+    if not direct:
+        for y in range(4):
+            for z in range(4):
+                for c in range(2):
+                    x=rest[0][(y*4+z)*2+c].astype(pa.dtype)
+                    pa[c,z,y]=x[0:64]
+                    pb[c,y,z]=x[64:128]
 def transpose_map(plan, F, w, dtype):
     o=SH((2,4,4,64,256),dtype)
     return pl.pallas_call(t_kernel,out_shape=(o,o),in_specs=[SM,VM,VM],out_specs=(VM,VM),
-        scratch_shapes=[pltpu.VMEM((33,128,256),f32),pltpu.VMEM((33,128,128),bf16),pltpu.VMEM((33,128,128),bf16)],
+        scratch_shapes=[pltpu.VMEM((33,128,128),bf16)]*2+([] if dtype==f32 else [pltpu.VMEM((32,128,256),f32)]),
         compiler_params=pltpu.CompilerParams(vmem_limit_bytes=24<<20), name="tmap")(plan,F,w)
 
 def f_kernel(plan, F, va, vb, img, acc):

time: 142 us -> 142 us (level)
  no operation moved by 1% of the time
where the time goes in v6:
time: 142 us
  Pallas kernels  137 us (96%)
  local copies, waits for them, and re-layouts  3.07 us (2%)
  other arithmetic  1.46 us (1%)
  between operations  1.42 us (1%)
    pallas_call x5, Pallas kernels, _call(): pl.pallas_call(kernel, out_shape=outs, in_specs=[VM] * len(args), out_spe...  120 us
    pallas_call x3, Pallas kernels, transpose_map(): pl.pallas_call(t_kernel, out_shape=(o, o), in_specs=[SM, VM, VM], out_spe...  10.1 us
    pallas_call x2, Pallas kernels, forward_map(): pl.pallas_call(f_kernel, out_shape=SH((32, 64, 128), bf16), in_specs=[SM,...  5.61 us
    unnamed x12, local copies, waits for them, and re-layouts  3.06 us

profile of v6, /device:TPU:1, one launch (start us, length us, event | category | flops | bytes accessed | tf_op | source)
XLA Modules:
  0.0 142.5 jit_solution(6485868293036037792)
XLA Ops:
  1.3 0.7 multiply_add_fusion.1
  2.0 0.0 slice-start
  2.0 0.0 copy-start
  2.0 0.0 copy-start.1
  2.0 0.0 copy-start.2
  2.0 0.0 slice-start.1
  2.0 0.0 slice-start.2
  2.1 0.5 sort.1.plan
  2.6 0.8 copy-done
  3.4 0.0 copy-done.1
  3.4 0.0 copy-done.2
  3.4 0.8 spread.1
  4.1 0.4 slice-done
  4.5 1.3 slice-done.1
  5.8 0.6 slice-done.2
  6.4 3.3 %tmap.3 = (f32[2,4,4,64,256]{4,3,2,1,0:T(8,128)S(1)}, f32[2,4,4,64,256]{4,3,2,1,0:T(8,128)S(1)}) custom-call(s32[2,512]{1,0:T(2,128)S(1)} %sort.1.plan, bf16[320,64,256]{2,1,0:T(8,128)(2,1)S(1)} %bitcast.18, bf16[32,64,128]{2,1,0:T(8,128)(2,1)S(1)} %get-tuple-element.32.w), custom_call_target="tpu_custom_call" | custom-call | tf_op jit(solution)/shard_map/tmap/pallas_call | solution.py:119
  9.7 37.7 %first.1 = (f32[256,128]{1,0:T(8,128)S(1)}, bf16[2,4,4,128,128]{4,3,2,1,0:T(8,128)(2,1)S(1)}, bf16[2,4,4,128,128]{4,3,2,1,0:T(8,128)(2,1)S(1)}, f32[8,128]{1,0:T(8,128)S(1)}) custom-call(f32[2,4,4,64,256]{4,3,2,1,0:T(8,128)S(1)} %get-tuple-element.33.pa, f32[2,4,4,64,256]{4,3,2,1,0:T(8,128)S(1)} %get-tuple-element.34.pb, f32[256,128]{1,0:T(8,128)S(1)} %get-tuple-element.31.prior), custom_call_target="tpu_custom_call" | custom-call | tf_op jit(solution)/shard_map/first/pallas_call | solution.py:414
  47.4 2.8 %fmap.2 = bf16[32,64,128]{2,1,0:T(8,128)(2,1)S(1)} custom-call(s32[2,512]{1,0:T(2,128)S(1)} %sort.1.plan, bf16[320,64,256]{2,1,0:T(8,128)(2,1)S(1)} %bitcast.18, bf16[2,16,128,128]{3,2,1,0:T(8,128)(2,1)S(1)} %bitcast.23, bf16[2,16,128,128]{3,2,1,0:T(8,128)(2,1)S(1)} %bitcast.24), custom_call_target="tpu_custom_call" | custom-call | tf_op jit(solution)/shard_map/fmap/pallas_call | solution.py:137
  50.2 19.3 %cross.1 = (bf16[4,8,64,128]{3,2,1,0:T(8,128)(2,1)S(1)}, f32[8,128]{1,0:T(8,128)S(1)}, f32[8,128]{1,0:T(8,128)S(1)}, f32[8,64,128]{2,1,0:T(8,128)S(1)}) custom-call(bf16[4,8,64,128]{3,2,1,0:T(8,128)(2,1)S(1)} %bitcast.20, f32[8,64,128]{2,1,0:T(8,128)S(1)} %get-tuple-element.37.wgt, f32[8,128]{1,0:T(8,128)S(1)} %get-tuple-element.38.part), custom_call_target="tpu_custom_call" | custom-call | tf_op jit(solution)/shard_map/cross/pallas_call | solution.py:414
  69.5 3.3 %tmap.4 = (f32[2,4,4,64,256]{4,3,2,1,0:T(8,128)S(1)}, f32[2,4,4,64,256]{4,3,2,1,0:T(8,128)S(1)}) custom-call(s32[2,512]{1,0:T(2,128)S(1)} %sort.1.plan, bf16[320,64,256]{2,1,0:T(8,128)(2,1)S(1)} %bitcast.18, bf16[32,64,128]{2,1,0:T(8,128)(2,1)S(1)} %bitcast.26), custom_call_target="tpu_custom_call" | custom-call | tf_op jit(solution)/shard_map/tmap/pallas_call | solution.py:119
  72.9 29.9 %mid.1 = (f32[256,128]{1,0:T(8,128)S(1)}, f32[256,128]{1,0:T(8,128)S(1)}, bf16[2,4,4,128,128]{4,3,2,1,0:T(8,128)(2,1)S(1)}, bf16[2,4,4,128,128]{4,3,2,1,0:T(8,128)(2,1)S(1)}, f32[8,128]{1,0:T(8,128)S(1)}) custom-call(f32[2,4,4,64,256]{4,3,2,1,0:T(8,128)S(1)} %get-tuple-element.40.pa, f32[2,4,4,64,256]{4,3,2,1,0:T(8,128)S(1)} %get-tuple-element.41.pb, ...), custom_call_target="tpu_custom_call" | custom-call | tf_op jit(solution)/shard_map/mid/pallas_call | solution.py:414
  102.7 2.8 %fmap.3 = bf16[32,64,128]{2,1,0:T(8,128)(2,1)S(1)} custom-call(s32[2,512]{1,0:T(2,128)S(1)} %sort.1.plan, bf16[320,64,256]{2,1,0:T(8,128)(2,1)S(1)} %bitcast.18, bf16[2,16,128,128]{3,2,1,0:T(8,128)(2,1)S(1)} %bitcast.21, bf16[2,16,128,128]{3,2,1,0:T(8,128)(2,1)S(1)} %bitcast.22), custom_call_target="tpu_custom_call" | custom-call | tf_op jit(solution)/shard_map/fmap/pallas_call | solution.py:137
  105.6 17.4 %again.1 = (bf16[4,8,64,128]{3,2,1,0:T(8,128)(2,1)S(1)}, f32[8,128]{1,0:T(8,128)S(1)}, f32[8,128]{1,0:T(8,128)S(1)}, f32[8,128]{1,0:T(8,128)S(1)}, f32[8,128]{1,0:T(8,128)S(1)}) custom-call(bf16[4,8,64,128]{3,2,1,0:T(8,128)(2,1)S(1)} %bitcast.19, f32[8,64,128]{2,1,0:T(8,128)S(1)} %get-tuple-element.37.wgt, f32[8,128]{1,0:T(8,128)S(1)} %get-tuple-element.48.part, ...), custom_call_target="tpu_custom_call" | custom-call | tf_op jit(solution)/shard_map/again/pallas_call | solution.py:414
  123.0 3.4 %tmap.5 = (bf16[2,4,4,64,256]{4,3,2,1,0:T(8,128)(2,1)S(1)}, bf16[2,4,4,64,256]{4,3,2,1,0:T(8,128)(2,1)S(1)}) custom-call(s32[2,512]{1,0:T(2,128)S(1)} %sort.1.plan, bf16[320,64,256]{2,1,0:T(8,128)(2,1)S(1)} %bitcast.18, bf16[32,64,128]{2,1,0:T(8,128)(2,1)S(1)} %bitcast.25), custom_call_target="tpu_custom_call" | custom-call | tf_op jit(solution)/shard_map/tmap/pallas_call | solution.py:119
  126.4 15.3 %last.1 = (f32[256,128]{1,0:T(8,128)S(1)}, f32[8,128]{1,0:T(8,128)S(1)}) custom-call(bf16[2,4,4,64,256]{4,3,2,1,0:T(8,128)(2,1)S(1)} %get-tuple-element.51.pa, bf16[2,4,4,64,256]{4,3,2,1,0:T(8,128)(2,1)S(1)} %get-tuple-element.52.pb, f32[8,128]{1,0:T(8,128)S(1)} %get-tuple-element.53.top, f32[8,128]{1,0:T(8,128)S(1)} %get-tuple-element.54.low, ...), custom_call_target="tpu_custom_call" | custom-call | tf_op jit(solution)/shard_map/last/pallas_call | solution.py:414
  141.7 0.8 subtract_bitcast_fusion
  (4 shorter events, 0.0 us)
Async XLA Ops:
  2.0 2.5 %slice-start = ((s8[10485760]{0:T(1024)(128)(4,1)}), s8[4194304]{0:T(1024)(128)(4,1)S(1)}, s32[]{:S(2)}) async-start(s8[10485760]{0:T(1024)(128)(4,1)} %bitcast.17), calls=%async_computation | async-start | bytes 8388608
  2.0 1.4 copy-start
  2.0 1.4 copy-start.1
  2.0 1.4 copy-start.2
  2.0 3.8 %slice-start.1 = ((s8[10485760]{0:T(1024)(128)(4,1)}), s8[4194304]{0:T(1024)(128)(4,1)S(1)}, s32[]{:S(2)}) async-start(s8[10485760]{0:T(1024)(128)(4,1)} %bitcast.17), calls=%async_computation.1 | async-start | bytes 8388608
  2.0 4.3 %slice-start.2 = ((s8[10485760]{0:T(1024)(128)(4,1)}), s8[2097152]{0:T(1024)(128)(4,1)S(1)}, s32[]{:S(2)}) async-start(s8[10485760]{0:T(1024)(128)(4,1)} %bitcast.17), calls=%async_computation.2 | async-start | bytes 4194304

commit v7 on v5

--- a/solution.py
+++ b/solution.py
@@ -425,7 +425,7 @@
     r0, va, vb, norm = first(pa, pb, prior)
     img = forward_map(plan, F, va, vb)
     w, norm, wi, image = cross(img, wgt, norm)
-    pa, pb = transpose_map(plan, F, w.reshape(32, 64, 128), f32)
+    pa, pb = transpose_map(plan, F, w.reshape(32, 64, 128), bf16)
     r1, it, va, vb, two = mid(pa, pb, prior, r0, norm, wi)
     img = forward_map(plan, F, va, vb)
     w, low, top, beta, wi = again(img, wgt, two, norm, image)

time: 142 us -> 142 us (level)
    pallas_call x5, Pallas kernels: 119 us -> 109 us  [_call(): pl.pallas_call(kernel, out_shape=outs, in_specs=[VM] * len(args), out_spe...]
    pallas_call x3, Pallas kernels: 10.3 us -> 15.8 us  [transpose_map(): pl.pallas_call(t_kernel, out_shape=(o, o), in_specs=[SM, VM, VM], out_spe...]
    pallas_call x2, Pallas kernels: 5.62 us -> 9.78 us  [forward_map(): pl.pallas_call(f_kernel, out_shape=SH((32, 64, 128), bf16), in_specs=[SM,...]
where the time goes in v7:
time: 142 us
  Pallas kernels  136 us (96%)
  local copies, waits for them, and re-layouts  3.07 us (2%)
  other arithmetic  1.45 us (1%)
  between operations  1.42 us (1%)
    pallas_call x5, Pallas kernels, _call(): pl.pallas_call(kernel, out_shape=outs, in_specs=[VM] * len(args), out_spe...  109 us
    pallas_call x3, Pallas kernels, transpose_map(): pl.pallas_call(t_kernel, out_shape=(o, o), in_specs=[SM, VM, VM], out_spe...  15.8 us
    pallas_call x2, Pallas kernels, forward_map(): pl.pallas_call(f_kernel, out_shape=SH((32, 64, 128), bf16), in_specs=[SM,...  9.78 us
    unnamed x12, local copies, waits for them, and re-layouts  3.06 us

profile of v7, /device:TPU:1, one launch (start us, length us, event | category | flops | bytes accessed | tf_op | source)
XLA Modules:
  0.0 141.8 jit_solution(661052452093731527)
XLA Ops:
  1.3 0.7 multiply_add_fusion.1
  2.0 0.0 slice-start
  2.0 0.0 copy-start
  2.0 0.0 copy-start.1
  2.0 0.0 copy-start.2
  2.0 0.0 slice-start.1
  2.0 0.0 slice-start.2
  2.1 0.5 sort.1.plan
  2.6 0.8 copy-done
  3.4 0.0 copy-done.1
  3.4 0.0 copy-done.2
  3.4 0.8 spread.1
  4.1 0.4 slice-done
  4.5 1.3 slice-done.1
  5.8 0.6 slice-done.2
  6.4 5.3 %tmap.3 = (f32[2,4,4,64,256]{4,3,2,1,0:T(8,128)S(1)}, f32[2,4,4,64,256]{4,3,2,1,0:T(8,128)S(1)}) custom-call(s32[2,512]{1,0:T(2,128)S(1)} %sort.1.plan, bf16[320,64,256]{2,1,0:T(8,128)(2,1)S(1)} %bitcast.18, bf16[32,64,128]{2,1,0:T(8,128)(2,1)S(1)} %get-tuple-element.32.w), custom_call_target="tpu_custom_call" | custom-call | tf_op jit(solution)/shard_map/tmap/pallas_call | solution.py:111
  11.7 36.9 %first.1 = (f32[256,128]{1,0:T(8,128)S(1)}, bf16[2,4,4,128,128]{4,3,2,1,0:T(8,128)(2,1)S(1)}, bf16[2,4,4,128,128]{4,3,2,1,0:T(8,128)(2,1)S(1)}, f32[8,128]{1,0:T(8,128)S(1)}) custom-call(f32[2,4,4,64,256]{4,3,2,1,0:T(8,128)S(1)} %get-tuple-element.33.pa, f32[2,4,4,64,256]{4,3,2,1,0:T(8,128)S(1)} %get-tuple-element.34.pb, f32[256,128]{1,0:T(8,128)S(1)} %get-tuple-element.31.prior), custom_call_target="tpu_custom_call" | custom-call | tf_op jit(solution)/shard_map/first/pallas_call | solution.py:406
  48.6 4.9 %fmap.2 = bf16[32,64,128]{2,1,0:T(8,128)(2,1)S(1)} custom-call(s32[2,512]{1,0:T(2,128)S(1)} %sort.1.plan, bf16[320,64,256]{2,1,0:T(8,128)(2,1)S(1)} %bitcast.18, bf16[2,16,128,128]{3,2,1,0:T(8,128)(2,1)S(1)} %bitcast.23, bf16[2,16,128,128]{3,2,1,0:T(8,128)(2,1)S(1)} %bitcast.24), custom_call_target="tpu_custom_call" | custom-call | tf_op jit(solution)/shard_map/fmap/pallas_call | solution.py:129
  53.5 15.3 %cross.1 = (bf16[4,8,64,128]{3,2,1,0:T(8,128)(2,1)S(1)}, f32[8,128]{1,0:T(8,128)S(1)}, f32[8,128]{1,0:T(8,128)S(1)}, f32[8,64,128]{2,1,0:T(8,128)S(1)}) custom-call(bf16[4,8,64,128]{3,2,1,0:T(8,128)(2,1)S(1)} %bitcast.20, f32[8,64,128]{2,1,0:T(8,128)S(1)} %get-tuple-element.37.wgt, f32[8,128]{1,0:T(8,128)S(1)} %get-tuple-element.38.part), custom_call_target="tpu_custom_call" | custom-call | tf_op jit(solution)/shard_map/cross/pallas_call | solution.py:406
  68.8 5.2 %tmap.4 = (bf16[2,4,4,64,256]{4,3,2,1,0:T(8,128)(2,1)S(1)}, bf16[2,4,4,64,256]{4,3,2,1,0:T(8,128)(2,1)S(1)}) custom-call(s32[2,512]{1,0:T(2,128)S(1)} %sort.1.plan, bf16[320,64,256]{2,1,0:T(8,128)(2,1)S(1)} %bitcast.18, bf16[32,64,128]{2,1,0:T(8,128)(2,1)S(1)} %bitcast.26), custom_call_target="tpu_custom_call" | custom-call | tf_op jit(solution)/shard_map/tmap/pallas_call | solution.py:111
  74.1 27.7 %mid.1 = (f32[256,128]{1,0:T(8,128)S(1)}, f32[256,128]{1,0:T(8,128)S(1)}, bf16[2,4,4,128,128]{4,3,2,1,0:T(8,128)(2,1)S(1)}, bf16[2,4,4,128,128]{4,3,2,1,0:T(8,128)(2,1)S(1)}, f32[8,128]{1,0:T(8,128)S(1)}) custom-call(bf16[2,4,4,64,256]{4,3,2,1,0:T(8,128)(2,1)S(1)} %get-tuple-element.40.pa, bf16[2,4,4,64,256]{4,3,2,1,0:T(8,128)(2,1)S(1)} %get-tuple-element.41.pb, ...), custom_call_target="tpu_custom_call" | custom-call | tf_op jit(solution)/shard_map/mid/pallas_call | solution.py:406
  101.8 4.9 %fmap.3 = bf16[32,64,128]{2,1,0:T(8,128)(2,1)S(1)} custom-call(s32[2,512]{1,0:T(2,128)S(1)} %sort.1.plan, bf16[320,64,256]{2,1,0:T(8,128)(2,1)S(1)} %bitcast.18, bf16[2,16,128,128]{3,2,1,0:T(8,128)(2,1)S(1)} %bitcast.21, bf16[2,16,128,128]{3,2,1,0:T(8,128)(2,1)S(1)} %bitcast.22), custom_call_target="tpu_custom_call" | custom-call | tf_op jit(solution)/shard_map/fmap/pallas_call | solution.py:129
  106.7 15.4 %again.1 = (bf16[4,8,64,128]{3,2,1,0:T(8,128)(2,1)S(1)}, f32[8,128]{1,0:T(8,128)S(1)}, f32[8,128]{1,0:T(8,128)S(1)}, f32[8,128]{1,0:T(8,128)S(1)}, f32[8,128]{1,0:T(8,128)S(1)}) custom-call(bf16[4,8,64,128]{3,2,1,0:T(8,128)(2,1)S(1)} %bitcast.19, f32[8,64,128]{2,1,0:T(8,128)S(1)} %get-tuple-element.37.wgt, f32[8,128]{1,0:T(8,128)S(1)} %get-tuple-element.48.part, ...), custom_call_target="tpu_custom_call" | custom-call | tf_op jit(solution)/shard_map/again/pallas_call | solution.py:406
  122.1 5.2 %tmap.5 = (bf16[2,4,4,64,256]{4,3,2,1,0:T(8,128)(2,1)S(1)}, bf16[2,4,4,64,256]{4,3,2,1,0:T(8,128)(2,1)S(1)}) custom-call(s32[2,512]{1,0:T(2,128)S(1)} %sort.1.plan, bf16[320,64,256]{2,1,0:T(8,128)(2,1)S(1)} %bitcast.18, bf16[32,64,128]{2,1,0:T(8,128)(2,1)S(1)} %bitcast.25), custom_call_target="tpu_custom_call" | custom-call | tf_op jit(solution)/shard_map/tmap/pallas_call | solution.py:111
  127.4 13.6 %last.1 = (f32[256,128]{1,0:T(8,128)S(1)}, f32[8,128]{1,0:T(8,128)S(1)}) custom-call(bf16[2,4,4,64,256]{4,3,2,1,0:T(8,128)(2,1)S(1)} %get-tuple-element.51.pa, bf16[2,4,4,64,256]{4,3,2,1,0:T(8,128)(2,1)S(1)} %get-tuple-element.52.pb, f32[8,128]{1,0:T(8,128)S(1)} %get-tuple-element.53.top, f32[8,128]{1,0:T(8,128)S(1)} %get-tuple-element.54.low, ...), custom_call_target="tpu_custom_call" | custom-call | tf_op jit(solution)/shard_map/last/pallas_call | solution.py:406
  141.0 0.7 subtract_bitcast_fusion
  (4 shorter events, 0.0 us)
Async XLA Ops:
  2.0 2.5 %slice-start = ((s8[10485760]{0:T(1024)(128)(4,1)}), s8[4194304]{0:T(1024)(128)(4,1)S(1)}, s32[]{:S(2)}) async-start(s8[10485760]{0:T(1024)(128)(4,1)} %bitcast.17), calls=%async_computation | async-start | bytes 8388608
  2.0 1.4 copy-start
  2.0 1.4 copy-start.1
  2.0 1.4 copy-start.2
  2.0 3.8 %slice-start.1 = ((s8[10485760]{0:T(1024)(128)(4,1)}), s8[4194304]{0:T(1024)(128)(4,1)S(1)}, s32[]{:S(2)}) async-start(s8[10485760]{0:T(1024)(128)(4,1)} %bitcast.17), calls=%async_computation.1 | async-start | bytes 8388608
  2.0 4.3 %slice-start.2 = ((s8[10485760]{0:T(1024)(128)(4,1)}), s8[2097152]{0:T(1024)(128)(4,1)S(1)}, s32[]{:S(2)}) async-start(s8[10485760]{0:T(1024)(128)(4,1)} %bitcast.17), calls=%async_computation.2 | async-start | bytes 4194304
